TPU v7x, 512 devices: a whole 4x4x16 slice. The times are simulated.
512 devices in a mesh: band: 128 (over z_lo, y, x, core), head: 4 (over z_hi).
Axes of the slice: x: 4, y: 4, z: 16 (z_hi: 4, z_lo: 4; z = z_hi * 4 + z_lo), core: 2. Of those that a mesh axis runs over, the one named last changes fastest.
Arguments:
- queries: bfloat16 [256, 131072], P('head', 'band'), may hold values from -76 to 76
- keys: bfloat16 [256, 131072], P('head', 'band'), may hold values from -6 to 6
- values: bfloat16 [256, 131072], P('head', 'band'), may hold values from -6 to 6
- grad_out: bfloat16 [256, 131072], P('head', 'band'), may hold values from -6 to 6
- w_out: bfloat16 [256, 256], P('head'), may hold values from -0.375 to 0.375
- key_lists: int32 [1024, 8], P('band'), may hold values from 0 to 1023, as said below
- key_counts: int32 [1024], P('band'), may hold values from 2 to 8, as said below
Outputs:
- grad_queries: bfloat16 [256, 131072], P('head', 'band')
- grad_keys: bfloat16 [256, 131072], P('head', 'band')
- grad_values: bfloat16 [256, 131072], P('head', 'band')
- grad_w_out: float32 [256, 256], P('head')
Inputs may be any that keep to these rules, and one draw needn't show every extreme that they name: `key_lists`: row b holds 8 different blocks; the first is b itself and every entry lies within 8 blocks of b. `key_counts`: the number of leading entries of the row of key_lists that are used.
All inputs are finite; a program needn't handle non-finite values.
Results may differ from a plain program's by a relative error of at most 0.0058.
Values may be sent and summed in bfloat16 or wider, within the bound.
A program may use at most 64 MiB of HBM per device.

v0:
```python
import jax
import jax.numpy as jnp
from jax import lax
from jax.sharding import PartitionSpec as P

HEAD_DIM = 32
BLOCK = 128
REACH = 4
MAX_KEYS = 8


def with_halo(block, sides, width):
    for axis, dim in sides:
        count = lax.axis_size(axis)
        forward = [(i, i + 1) for i in range(count - 1)]
        backward = [(target, source) for source, target in forward]
        low = lax.ppermute(
            lax.slice_in_dim(block, block.shape[dim] - width, None, axis=dim), axis, forward
        )
        high = lax.ppermute(lax.slice_in_dim(block, 0, width, axis=dim), axis, backward)
        block = jnp.concatenate([low, block, high], axis=dim)
    return block


def shifted(value, axis, steps):
    count = lax.axis_size(axis)
    initial, last = (max(0, -steps), min(count, count - steps))
    return lax.ppermute(value, axis, [(source, source + steps) for source in range(initial, last)])


def block_grads(query_blk, grad_blk, slots, usable, key_ext, value_ext, bias_ext):
    count = slots.shape[0]
    span = count * BLOCK
    chans = query_blk.shape[0]
    heads_here = chans // HEAD_DIM
    scale = HEAD_DIM ** (-0.5)
    picked_k = key_ext[:, slots].reshape(heads_here, HEAD_DIM, span)
    picked_v = value_ext[:, slots].reshape(heads_here, HEAD_DIM, span)
    key_bias = bias_ext[slots].reshape(span)
    live_keys = jnp.repeat(usable, BLOCK)
    query_h = query_blk.reshape(heads_here, HEAD_DIM, BLOCK)
    grad_h = grad_blk.reshape(heads_here, HEAD_DIM, BLOCK)
    scores = (
        jnp.einsum("hdq,hdk->hqk", query_h, picked_k, preferred_element_type=jnp.float32) * scale
        + key_bias
    )
    scores = jnp.where(live_keys, scores, -jnp.inf)
    peak = jnp.max(scores, axis=-1)
    log_total = peak + jnp.log(jnp.sum(jnp.exp(scores - peak[..., None]), axis=-1))
    probs = jnp.exp(scores - log_total[..., None])
    probs_low = probs.astype(jnp.bfloat16)
    dprobs = jnp.einsum("hdq,hdk->hqk", grad_h, picked_v, preferred_element_type=jnp.float32)
    spread = jnp.sum(probs * dprobs, axis=-1)
    dscores = (probs * (dprobs - spread[..., None]) * scale).astype(jnp.bfloat16)
    dquery = jnp.einsum(
        "hqk,hdk->hdq", dscores, picked_k, preferred_element_type=jnp.float32
    ).reshape(chans, BLOCK)
    dkey = jnp.einsum("hqk,hdq->hdk", dscores, query_h, preferred_element_type=jnp.float32).reshape(
        chans, count, BLOCK
    )
    dvalue = jnp.einsum(
        "hqk,hdq->hdk", probs_low, grad_h, preferred_element_type=jnp.float32
    ).reshape(chans, count, BLOCK)
    attended = jnp.einsum(
        "hqk,hdk->hdq", probs_low, picked_v, preferred_element_type=jnp.float32
    ).reshape(chans, BLOCK)
    return (dquery, dkey, dvalue, attended, log_total, spread)


def band_bias(first_block, ext_blocks, total_tokens):
    positions = first_block * BLOCK + jnp.arange(ext_blocks * BLOCK, dtype=jnp.int32)
    positions = jnp.clip(positions, 0, total_tokens - 1).astype(jnp.float32)
    return jnp.log(jnp.sin(jnp.pi * (positions + 0.5) / total_tokens)).reshape(ext_blocks, BLOCK)


def run_blocks(query_blocks, grad_blocks, slot_rows, use_rows, key_ext, value_ext, bias_ext):
    chans = query_blocks.shape[0]
    nblocks = query_blocks.shape[1]
    heads_here = chans // HEAD_DIM
    ext_blocks = key_ext.shape[1]
    zeros = jnp.zeros((chans, ext_blocks, BLOCK), jnp.float32)
    start = (
        zeros,
        zeros,
        jnp.zeros((chans, nblocks, BLOCK), jnp.bfloat16),
        jnp.zeros((chans, nblocks, BLOCK), jnp.bfloat16),
        jnp.zeros((nblocks, heads_here, BLOCK), jnp.float32),
        jnp.zeros((nblocks, heads_here, BLOCK), jnp.float32),
    )

    def run_width(index, carry):
        acc_k, acc_v, dq_all, att_all, lse_all, spread_all = carry
        query_blk = lax.dynamic_index_in_dim(query_blocks, index, 1, keepdims=False)
        grad_blk = lax.dynamic_index_in_dim(grad_blocks, index, 1, keepdims=False)
        slots = slot_rows[index]
        dquery, dkey, dvalue, attended, log_total, spread = block_grads(
            query_blk, grad_blk, slots, use_rows[index], key_ext, value_ext, bias_ext
        )
        acc_k = acc_k.at[:, slots].add(dkey)
        acc_v = acc_v.at[:, slots].add(dvalue)
        dq_all = dq_all.at[:, index].set(dquery.astype(jnp.bfloat16))
        att_all = att_all.at[:, index].set(attended.astype(jnp.bfloat16))
        lse_all = lse_all.at[index].set(log_total)
        spread_all = spread_all.at[index].set(spread)
        return (acc_k, acc_v, dq_all, att_all, lse_all, spread_all)

    def block_step(index, carry):
        return run_width(index, carry)

    return lax.fori_loop(0, nblocks, block_step, start)


def shards(queries, keys, values, grad_out, w_out, key_lists, key_counts):
    chans = queries.shape[0]
    blocks = queries.shape[1] // BLOCK
    rim_blocks = 2 * REACH
    ext_blocks = blocks + 2 * rim_blocks
    band_index = lax.axis_index("band")
    band_count = lax.axis_size("band")
    total_tokens = blocks * BLOCK * band_count
    full_grad = lax.all_gather(grad_out, "head", axis=0, tiled=True)
    grad_att = jnp.einsum("cd,dt->ct", w_out, full_grad, preferred_element_type=jnp.float32).astype(
        jnp.bfloat16
    )
    key_pairs = jnp.stack(
        [keys.reshape(chans, blocks, BLOCK), values.reshape(chans, blocks, BLOCK)]
    )
    pair_ext = with_halo(key_pairs, (("band", 2),), rim_blocks)
    key_ext = pair_ext[0]
    value_ext = pair_ext[1]
    first_block = band_index * blocks - rim_blocks
    bias_ext = band_bias(first_block, ext_blocks, total_tokens)
    slot_ids = jnp.arange(MAX_KEYS, dtype=jnp.int32)
    masked = jnp.where(slot_ids[None, :] < key_counts[:, None], key_lists, -1)
    usable = masked >= 0
    local_slots = jnp.clip(masked - first_block, 0, ext_blocks - 1)
    query_blocks = queries.reshape(chans, blocks, BLOCK)
    grad_blocks = grad_att.reshape(chans, blocks, BLOCK)
    acc_k, acc_v, dq_all, att_all, lse_all, spread_all = run_blocks(
        query_blocks, grad_blocks, local_slots, usable, key_ext, value_ext, bias_ext
    )
    lower_part = jnp.stack([acc_k[:, :rim_blocks], acc_v[:, :rim_blocks]])
    upper_part = jnp.stack([acc_k[:, rim_blocks + blocks :], acc_v[:, rim_blocks + blocks :]])
    from_above = shifted(lower_part.astype(jnp.bfloat16), "band", -1).astype(lower_part.dtype)
    from_below = shifted(upper_part.astype(jnp.bfloat16), "band", 1).astype(upper_part.dtype)
    owned = jnp.stack(
        [acc_k[:, rim_blocks : rim_blocks + blocks], acc_v[:, rim_blocks : rim_blocks + blocks]]
    )
    owned = owned.at[:, :, :rim_blocks].add(from_below)
    owned = owned.at[:, :, blocks - rim_blocks :].add(from_above)
    grad_queries = dq_all.reshape(chans, blocks * BLOCK)
    grad_keys = owned[0].reshape(chans, blocks * BLOCK).astype(jnp.bfloat16)
    grad_values = owned[1].reshape(chans, blocks * BLOCK).astype(jnp.bfloat16)
    attended = att_all.reshape(chans, blocks * BLOCK)
    partial_w = jnp.einsum("ct,dt->cd", attended, full_grad, preferred_element_type=jnp.float32)
    grad_w_out = lax.psum(partial_w, "band")
    return (grad_queries, grad_keys, grad_values, grad_w_out)


def solution(mesh):
    in_specs = (
        P("head", "band"),
        P("head", "band"),
        P("head", "band"),
        P("head", "band"),
        P("head", None),
        P("band", None),
        P("band"),
    )
    out_specs = (P("head", "band"), P("head", "band"), P("head", "band"), P("head", None))
    return jax.shard_map(shards, mesh=mesh, in_specs=in_specs, out_specs=out_specs, check_vma=False)
```

profile of v0, /device:TPU:1, one launch (start us, length us, event | category | flops | bytes accessed | tf_op | source)
XLA Modules:
  0.0 1362.8 jit_solution(3524123765928324000)
XLA Ops:
  9.2 8.7 collective-permute-start.1
  18.0 1.9 collective-permute-start
  21.3 27.2 %all_gather.3 = bf16[256,1024]{1,0:T(8,128)(2,1)S(1)} all-gather(bf16[64,1024]{1,0:T(8,128)(2,1)S(1)} %copy-done.10), channel_id=1, replica_groups=mesh['band'=128,'head'=4] {'head'}, dimensions={0}, use_global_device_ids=true | all-gather | bytes 655360 | tf_op jit(solution)/shard_map/all_gather | solution.py:121
  53.1 139.8 %while.26 = (s32[]{:T(128)}, f32[64,24,128]{2,0,1:T(8,128)}, f32[64,24,128]{2,0,1:T(8,128)S(1)}, bf16[64,8,128]{2,0,1:T(8,128)(2,1)S(1)}, bf16[64,8,128]{2,0,1:T...) while((s32[]{:T(128)}, f32[64,24,128]{2,0,1:T(8,128)}, ...), condition=%wide.region_7.8_spmd.clone, body=%wide.region_0.7_spmd.clone.sunk | while | flops 107143464 | bytes 23508944 | solution.py:110
  57.3 1.6 gather_fusion.2
  59.1 1.6 gather_fusion
  64.8 1.8 fusion.90
  66.7 2.0 constant_dynamic-update-slice_fusion.3
  70.6 1.4 and_reduce_fusion.2
  74.8 1.6 gather_fusion.2
  76.5 1.6 gather_fusion
  82.2 1.8 fusion.90
  84.2 2.0 constant_dynamic-update-slice_fusion.3
  88.0 1.4 and_reduce_fusion.2
  92.3 1.6 gather_fusion.2
  94.0 1.6 gather_fusion
  99.7 1.8 fusion.90
  101.7 2.0 constant_dynamic-update-slice_fusion.3
  105.5 1.4 and_reduce_fusion.2
  109.7 1.6 gather_fusion.2
  111.5 1.6 gather_fusion
  117.2 1.8 fusion.90
  119.2 2.0 constant_dynamic-update-slice_fusion.3
  123.0 1.4 and_reduce_fusion.2
  127.2 1.6 gather_fusion.2
  129.0 1.6 gather_fusion
  134.7 1.8 fusion.90
  136.6 2.0 constant_dynamic-update-slice_fusion.3
  140.5 1.4 and_reduce_fusion.2
  144.7 1.6 gather_fusion.2
  146.5 1.6 gather_fusion
  152.2 1.8 fusion.90
  154.1 2.0 constant_dynamic-update-slice_fusion.3
  158.0 1.4 and_reduce_fusion.2
  162.2 1.6 gather_fusion.2
  163.9 1.6 gather_fusion
  169.6 1.8 fusion.90
  171.6 2.0 constant_dynamic-update-slice_fusion.3
  175.4 1.4 and_reduce_fusion.2
  179.7 1.6 gather_fusion.2
  181.4 1.6 gather_fusion
  187.1 1.8 fusion.90
  189.1 2.0 constant_dynamic-update-slice_fusion.3
  192.9 2.1 fusion.34
  195.3 2.4 collective-permute-start.3
  197.8 4.7 collective-permute-start.2
  207.4 1147.0 %all-reduce.2.cloned.1.call-done = f32[64,256]{1,0:T(8,128)} async-done(((f32[64,256]{1,0:T(8,128)}), f32[64,256]{1,0:T(8,128)}) %all-reduce.2.cloned.1.call-update) | async-done | bytes 65552 | tf_op jit(solution)/shard_map/psum | solution.py:156
  1354.4 1.5 copy.98
  (395 shorter events, 85.5 us)
Async XLA Ops:
  7.2 41.5 %copy-start = (bf16[64,1024]{1,0:T(8,128)(2,1)S(1)}, bf16[64,1024]{1,0:T(8,128)(2,1)}, u32[]{:S(2)}) copy-start(bf16[64,1024]{1,0:T(8,128)(2,1)} %param.21) | copy-start | bytes 393220
  7.2 12.7 copy-start.15
  7.2 12.7 copy-start.14
  7.2 14.1 %copy-start.10 = (bf16[64,1024]{1,0:T(8,128)(2,1)S(1)}, bf16[64,1024]{1,0:T(8,128)(2,1)}, u32[]{:S(2)}) copy-start(bf16[64,1024]{1,0:T(8,128)(2,1)} %param.24) | copy-start | bytes 393220
  7.2 41.2 %copy-start.13 = (bf16[64,256]{1,0:T(8,128)(2,1)S(1)}, bf16[64,256]{1,0:T(8,128)(2,1)}, u32[]{:S(2)}) copy-start(bf16[64,256]{1,0:T(8,128)(2,1)} %param.25) | copy-start | bytes 98308
  7.2 1347.2 %all-reduce.2.cloned.1.call-start = ((), (), s32[]{:S(2)}) async-start(), calls=%async_computation | async-start | bytes 131072 | tf_op jit(solution)/shard_map/psum | solution.py:156
  9.2 40.1 %collective-permute-start.1 = (bf16[2,64,8,128]{3,2,1,0:T(8,128)(2,1)S(1)}, bf16[2,64,8,128]{3,2,1,0:T(8,128)(2,1)S(1)}, u32[]{:S(2)}, u32[]{:S(2)}) collective-permute-start(bf16[2,64,8,128]{3,2,1,0:T(8,128)(2,1)S(1)} %bitcast_dynamic-update-slice_fusion), channel_id=1, source_target_pairs={{4,0},{8,4},{12,8},{16,12},{20,16},{24,20},{28,24},{32,28},{36,32}... | collective-permute-start | bytes 786440 | tf_op jit(solution)/shard_map/ppermute | solution.py:20
  18.0 31.4 %collective-permute-start = (bf16[2,64,8,128]{3,2,1,0:T(8,128)(2,1)S(1)}, bf16[2,64,8,128]{3,2,1,0:T(8,128)(2,1)S(1)}, u32[]{:S(2)}, u32[]{:S(2)}) collective-permute-start(bf16[2,64,8,128]{3,2,1,0:T(8,128)(2,1)S(1)} %bitcast_dynamic-update-slice_fusion), channel_id=1, source_target_pairs={{0,4},{4,8},{8,12},{12,16},{16,20},{20,24},{24,28},{28,32},{32,36}... | collective-permute-start | bytes 786440 | tf_op jit(solution)/shard_map/ppermute | solution.py:17
  53.1 5.8 copy-start.7
  55.2 7.3 copy-start.11
  57.3 3.9 copy-start.5
  64.8 4.0 copy-start.12
  66.7 3.9 copy-start.8
  70.6 5.8 copy-start.7
  72.6 7.3 copy-start.11
  74.8 3.9 copy-start.5
  82.2 4.0 copy-start.12
  84.1 3.9 copy-start.8
  88.0 5.8 copy-start.7
  90.1 7.3 copy-start.11
  92.3 3.9 copy-start.5
  99.7 4.0 copy-start.12
  101.6 3.9 copy-start.8
  105.5 5.8 copy-start.7
  107.6 7.3 copy-start.11
  109.7 3.9 copy-start.5
  117.2 4.0 copy-start.12
  119.1 3.9 copy-start.8
  123.0 5.8 copy-start.7
  125.1 7.3 copy-start.11
  127.2 3.9 copy-start.5
  134.7 4.0 copy-start.12
  136.6 3.9 copy-start.8
  140.5 5.8 copy-start.7
  142.5 7.3 copy-start.11
  144.7 3.9 copy-start.5
  152.1 4.0 copy-start.12
  154.0 3.9 copy-start.8
  157.9 5.8 copy-start.7
  160.0 7.3 copy-start.11
  162.2 3.9 copy-start.5
  169.6 4.0 copy-start.12
  175.4 5.8 copy-start.7
  177.5 7.3 copy-start.11
  179.6 3.9 copy-start.5
  187.1 4.0 copy-start.12
  195.3 9.2 collective-permute-start.3
  197.8 8.0 collective-permute-start.2
  (36 other events, 61.1 us)
Sparse Core Ops, SparseCore 0:
  195.1 1159.2 all-reduce.1
where the time goes:
time: 1370 us; the launch traced here: 1360 us
  waiting for transfers between devices  1150 us (84%)
  local copies, waits for them, and re-layouts  63.2 us (5%)
  other arithmetic  51.8 us (4%)
  matrix products  37.2 us (3%)
  blocking collectives  27.2 us (2%)
  starting transfers between devices  17.8 us (1%)
  between operations  14.3 us (1%)
    psum x1, waiting for transfers between devices, shards(): grad_w_out = lax.psum(partial_w, 'band')  1150 us
  transfers between devices with their start and end apart: 5, of which 3 were waited for; matrix products, arithmetic and copies ran while one was open for 0% of the time, Pallas kernels for 0%

commit v1 on v0

v1 whole, which is shorter than its diff:
```python
import math
import jax
import jax.numpy as jnp
from jax import lax
from jax.experimental import pallas as pl
from jax.experimental.pallas import tpu as pltpu
from jax.sharding import PartitionSpec as P

MESH = pl.DeviceIdType.MESH

def coords():
    me = lax.axis_index("band")
    core = lax.rem(me, 2); x = lax.rem(me // 2, 4); y = lax.rem(me // 8, 4); z = me // 32
    return core, x, y, z

def band_of(core, x, y, z):
    return ((z * 4 + y) * 4 + x) * 2 + core

def ar_kernel(w_ref, o_ref, part, r1, red, r2, tot, gat, s1, q1, s2, q2, s3, q3):
    core, x, y, z = coords()
    a = y * 4 + x
    plane = [(d, band_of(core, lax.rem(x + d % 4, 4), lax.rem(y + d // 4, 4), z),
              lax.rem(y + d // 4, 4) * 4 + lax.rem(x + d % 4, 4)) for d in range(1, 16)]
    line = [(d, band_of(lax.rem(core + d % 2, 2), x, y, lax.rem(z + d // 2, 4))) for d in range(1, 8)]
    barrier = pltpu.get_barrier_semaphore()
    for _, b, _ in plane:
        pl.semaphore_signal(barrier, inc=1, device_id={"band": b}, device_id_type=MESH)
    for _, b in line:
        pl.semaphore_signal(barrier, inc=1, device_id={"band": b}, device_id_type=MESH)
    w = w_ref[...]
    for t in range(16):
        part[t] = w[(t // 2) * 8:(t // 2) * 8 + 8, (t % 2) * 128:(t % 2) * 128 + 128]
    pl.semaphore_wait(barrier, 22)
    c1 = []
    for d, b, pa in plane:
        c = pltpu.make_async_remote_copy(src_ref=part.at[pa], dst_ref=r1.at[d], send_sem=s1.at[d], recv_sem=q1.at[d],
                                         device_id={"band": b}, device_id_type=MESH)
        c.start(); c1.append(c)
    for c in c1:
        c.wait_recv()
    acc = part[a]
    for d in range(1, 16):
        acc = acc + r1[d]
    red[...] = acc
    c2 = []
    for d, b in line:
        c = pltpu.make_async_remote_copy(src_ref=red, dst_ref=r2.at[d], send_sem=s2.at[d], recv_sem=q2.at[d],
                                         device_id={"band": b}, device_id_type=MESH)
        c.start(); c2.append(c)
    for c in c2:
        c.wait_recv()
    for d in range(1, 8):
        acc = acc + r2[d]
    tot[...] = acc
    gat[a] = acc
    c3 = []
    for d, b, pa in plane:
        c = pltpu.make_async_remote_copy(src_ref=tot, dst_ref=gat.at[a], send_sem=s3.at[d], recv_sem=q3.at[d],
                                         device_id={"band": b}, device_id_type=MESH)
        c.start(); c3.append(c)
    for c in c3:
        c.wait_recv()
    for t in range(16):
        o_ref[(t // 2) * 8:(t // 2) * 8 + 8, (t % 2) * 128:(t % 2) * 128 + 128] = gat[t]
    for c in c1 + c2 + c3:
        c.wait_send()

def ar(w):
    D = pltpu.SemaphoreType.DMA
    return pl.pallas_call(
        ar_kernel, out_shape=jax.ShapeDtypeStruct((64, 256), jnp.float32),
        in_specs=[pl.BlockSpec(memory_space=pltpu.VMEM)], out_specs=pl.BlockSpec(memory_space=pltpu.VMEM),
        scratch_shapes=[pltpu.VMEM((16, 8, 128), jnp.float32), pltpu.VMEM((16, 8, 128), jnp.float32), pltpu.VMEM((8, 128), jnp.float32),
                        pltpu.VMEM((8, 8, 128), jnp.float32), pltpu.VMEM((8, 128), jnp.float32), pltpu.VMEM((16, 8, 128), jnp.float32),
                        D((16,)), D((16,)), D((8,)), D((8,)), D((16,)), D((16,))],
        compiler_params=pltpu.CompilerParams(collective_id=0, has_side_effects=True),
        name="band_sum")(w)

SCALE = 32 ** -0.5
C = SCALE * math.log2(math.e)
F32, BF16 = jnp.float32, jnp.bfloat16

def dot(a, b):
    return jnp.dot(a, b, preferred_element_type=F32)

def dot_nt(a, b):
    return lax.dot_general(a, b, (((1,), (1,)), ((), ())), preferred_element_type=F32)

def fold(x):
    return x.reshape(16, 8, 256)

def head_diag(m):
    return jnp.concatenate([m[0:32, 0:128], m[32:64, 128:256]], axis=0)

def block_diag(m):
    z = jnp.zeros((32, 128), m.dtype)
    top = jnp.concatenate([m[0:32], z], axis=1)
    low = jnp.concatenate([z, m[32:64]], axis=1)
    return jnp.concatenate([top, low], axis=0)

def prep_block(e, k, v, bias_row, kv_fm, k_tm, v_tm):
    kv_fm[e, 0:64] = k
    kv_fm[e, 64:128] = v
    hi = bias_row.astype(BF16).astype(F32)
    mid = (bias_row - hi).astype(BF16).astype(F32)
    lo = (bias_row - hi) - mid
    row = lax.broadcasted_iota(jnp.int32, (64, 128), 0)
    aug = jnp.where(row == 0, hi, jnp.where(row == 1, mid, jnp.where(row == 2, lo, 0.0))).astype(BF16)
    k_tm[e] = jnp.concatenate([k, aug], axis=0).T
    v_tm[e] = jnp.concatenate([v, jnp.zeros((64, 128), BF16)], axis=0).T

def forward_block(b, q, eidx, kv_fm, k_tm, s_ref, p_ref, ps, inv_ref):
    qd = block_diag(q)
    qa = jnp.concatenate([qd, jnp.ones((64, 256), BF16)], axis=0)
    es = [eidx[b * 8 + j] for j in range(8)]
    top = None
    for j in range(8):
        s = dot(k_tm[es[j]], qa)
        s_ref[j] = s
        m8 = jnp.max(s.reshape(16, 8, 256), axis=0)
        top = m8 if top is None else jnp.maximum(top, m8)
    top = jnp.max(top, axis=0, keepdims=True) * C
    total = None
    for j in range(8):
        p = jnp.exp2(s_ref[j] * C - top)
        p_ref[b * 8 + j] = p
        l8 = jnp.sum(p.reshape(16, 8, 256), axis=0)
        total = l8 if total is None else total + l8
    inv = 1.0 / jnp.sum(total, axis=0, keepdims=True)
    inv_ref[b] = inv
    for j in range(8):
        ps[b * 8 + j, :, 256:512] = (p_ref[b * 8 + j] * inv).astype(BF16)
    v_all = jnp.concatenate([kv_fm[es[j], 64:128] for j in range(8)], axis=1)
    p_all = ps[pl.ds(b * 8, 8), :, 256:512].reshape(1024, 256)
    return head_diag(dot(v_all, p_all)).astype(BF16)

def backward_block(b, q, g, eidx, inv_idx, kv_fm, v_tm, d_ref, p_ref, ps, inv_ref, acc):
    gd = block_diag(g)
    ga = jnp.concatenate([gd, jnp.zeros((64, 256), BF16)], axis=0)
    es = [eidx[b * 8 + j] for j in range(8)]
    tot = None
    for j in range(8):
        d = dot(v_tm[es[j]], ga)
        d_ref[j] = d
        t8 = jnp.sum((p_ref[b * 8 + j] * d).reshape(16, 8, 256), axis=0)
        tot = t8 if tot is None else tot + t8
    inv = inv_ref[b]
    spread = jnp.sum(tot, axis=0, keepdims=True) * inv
    isc = inv * SCALE
    for j in range(8):
        ps[b * 8 + j, :, 0:256] = ((p_ref[b * 8 + j] * isc) * (d_ref[j] - spread)).astype(BF16)
    k_all = jnp.concatenate([kv_fm[es[j], 0:64] for j in range(8)], axis=1)
    d_all = ps[pl.ds(b * 8, 8), :, 0:256].reshape(1024, 256)
    dq = head_diag(dot(k_all, d_all)).astype(BF16)
    z = jnp.zeros((64, 256), BF16)
    w = jnp.concatenate([jnp.concatenate([block_diag(q), z], axis=1), jnp.concatenate([z, gd], axis=1)], axis=0)
    for i in range(17):
        acc[b + i] += dot_nt(ps[inv_idx[b * 17 + i]], w)
    return dq

def attn_kernel(eidx, inv_idx, bias, q_ref, kv_ref, grad_ref, w_out, dq_ref, acc, pw_ref,
                kv_fm, k_tm, v_tm, s_ref, p_ref, ps, inv_ref, att_ref):
    for e in range(24):
        prep_block(e, kv_ref[e // 8, 0, :, (e % 8) * 128:(e % 8 + 1) * 128], kv_ref[e // 8, 1, :, (e % 8) * 128:(e % 8 + 1) * 128],
                   bias[e:e + 1], kv_fm, k_tm, v_tm)
    zero = jnp.zeros((64, 128), BF16)
    prep_block(24, zero, zero, jnp.full((1, 128), -1e30, F32), kv_fm, k_tm, v_tm)
    ps[64] = jnp.zeros((128, 512), BF16)
    acc[...] = jnp.zeros_like(acc)

    def fwd(b, _):
        cols = pl.ds(pl.multiple_of(b * 128, 128), 128)
        att_ref[:, cols] = forward_block(b, q_ref[:, cols], eidx, kv_fm, k_tm, s_ref, p_ref, ps, inv_ref)
        return 0
    lax.fori_loop(0, 8, fwd, 0)

    def bwd(b, _):
        cols = pl.ds(pl.multiple_of(b * 128, 128), 128)
        g = dot(w_out[...], grad_ref[:, cols]).astype(BF16)
        dq_ref[:, cols] = backward_block(b, q_ref[:, cols], g, eidx, inv_idx, kv_fm, v_tm, s_ref, p_ref, ps, inv_ref, acc)
        return 0
    lax.fori_loop(0, 8, bwd, 0)
    pw_ref[...] = dot_nt(att_ref[...], grad_ref[...])

def attn(eidx, inv_idx, bias, q, kv, grad, w_out):
    V = pltpu.VMEM
    vs = pl.BlockSpec(memory_space=V)
    ss = pl.BlockSpec(memory_space=pltpu.SMEM)
    return pl.pallas_call(
        attn_kernel,
        out_shape=(jax.ShapeDtypeStruct((64, 1024), BF16), jax.ShapeDtypeStruct((24, 128, 128), F32), jax.ShapeDtypeStruct((64, 256), F32)),
        in_specs=[ss, ss, vs, vs, vs, vs, vs], out_specs=(vs, vs, vs),
        scratch_shapes=[V((25, 128, 128), BF16), V((25, 128, 128), BF16), V((25, 128, 128), BF16), V((8, 128, 256), F32),
                        V((64, 128, 256), F32), V((65, 128, 512), BF16), V((8, 1, 256), F32), V((64, 1024), BF16)],
        compiler_params=pltpu.CompilerParams(vmem_limit_bytes=60 * 2**20),
        name="attention_grads")(eidx, inv_idx, bias, q, kv, grad, w_out)


def shifted(value, steps):
    count = lax.axis_size("band")
    first, last = max(0, -steps), min(count, count - steps)
    return lax.ppermute(value, "band", [(i, i + steps) for i in range(first, last)])


def tables(key_lists, key_counts):
    first = lax.axis_index("band") * 8 - 8
    used = jnp.arange(8, dtype=jnp.int32)[None, :] < key_counts[:, None]
    local = key_lists - first
    eidx = jnp.where(used, local, 24)
    rows = jnp.arange(8, dtype=jnp.int32)[:, None]
    offset = jnp.where(used, local - rows, -1)
    hit = offset[:, None, :] == jnp.arange(17, dtype=jnp.int32)[None, :, None]
    tile = (rows * 8 + jnp.arange(8, dtype=jnp.int32)[None, :])[:, None, :]
    inv_idx = jnp.min(jnp.where(hit, tile, 64), axis=2)
    positions = first * 128 + jnp.arange(3072, dtype=jnp.int32)
    total = 1024 * lax.axis_size("band")
    positions = jnp.clip(positions, 0, total - 1).astype(jnp.float32)
    bias = jnp.log(jnp.sin(jnp.pi * (positions + 0.5) / total)).reshape(24, 128) * (32 ** 0.5)
    return eidx.reshape(-1), inv_idx.reshape(-1), bias


def shards(queries, keys, values, grad_out, w_out, key_lists, key_counts):
    full_grad = lax.all_gather(grad_out, "head", axis=0, tiled=True)
    pair = jnp.stack([keys, values])
    kv = jnp.stack([shifted(pair, 1), pair, shifted(pair, -1)])
    eidx, inv_idx, bias = tables(key_lists, key_counts)
    grad_queries, acc, partial_w = attn(eidx, inv_idx, bias, queries, kv, full_grad, w_out)
    grad_w_out = ar(partial_w)
    from_above = shifted(acc[:8].astype(BF16), -1).astype(F32)
    from_below = shifted(acc[16:].astype(BF16), 1).astype(F32)
    own = (acc[8:16] + from_above + from_below).astype(BF16)
    both = own.transpose(2, 0, 1).reshape(128, 1024)
    return grad_queries, both[:64], both[64:], grad_w_out


def solution(mesh):
    split = P("head", "band")
    in_specs = (split, split, split, split, P("head", None), P("band", None), P("band"))
    out_specs = (split, split, split, P("head", None))
    return jax.shard_map(shards, mesh=mesh, in_specs=in_specs, out_specs=out_specs, check_vma=False)
```

time: 1370 us -> 103 us (0.08)
  waiting for transfers between devices: 1150 us -> 0.01 us
  local copies, waits for them, and re-layouts: 63.2 us -> 3.67 us
  Pallas kernels: 0 us -> 46.2 us
  other arithmetic: 51.8 us -> 6.2 us
  matrix products: 37.2 us -> 0 us
    psum x1 -> x0, waiting for transfers between devices: 1150 us -> none  [shards(): grad_w_out = lax.psum(partial_w, 'band')]
    pallas_call x0 -> x2, Pallas kernels: none -> 46.2 us  [the longest x1 24.6 us: ar(): pl.pallas_call(ar_kernel, out_shape=jax.ShapeDtypeStruct((64, 256), jnp.f...]
    dot_general x50 -> x0, matrix products: 37.2 us -> none  [the longest x8 14.6 us: block_grads(): jnp.einsum('hqk,hdq->hdk', dscores, query_h, preferred_element_type=jnp.f...]
    gather x40 -> x0, local copies, waits for them, and re-layouts: 31 us -> none  [the longest x16 13.3 us: block_grads(): picked_k = key_ext[:, slots].reshape(heads_here, HEAD_DIM, span)]
    scatter x8 -> x0, other arithmetic: 16.3 us -> none  [run_width(): att_all = att_all.at[:, index].set(attended.astype(jnp.bfloat16))]
    scatter-add x16 -> x0, other arithmetic: 14.2 us -> none  [the longest x8 7.1 us: run_width(): acc_v = acc_v.at[:, slots].add(dvalue)]
  transfers between devices with their start and end apart: 5 -> 4, of which waited for: 3 -> 0; matrix products, arithmetic and copies ran while one was open for 0% -> 3% of each run, Pallas kernels for 0% -> 24%
where the time goes in v1:
time: 103 us
  Pallas kernels  46.2 us (45%)
  blocking collectives  29.8 us (29%)
  starting transfers between devices  16.2 us (16%)
  other arithmetic  6.2 us (6%)
  local copies, waits for them, and re-layouts  3.67 us (4%)
    all_gather x1, blocking collectives, shards(): full_grad = lax.all_gather(grad_out, 'head', axis=0, tiled=True)  29.8 us
    pallas_call x1, Pallas kernels, ar(): pl.pallas_call(ar_kernel, out_shape=jax.ShapeDtypeStruct((64, 256), jnp.f...  24.6 us
    pallas_call x1, Pallas kernels, attn(): pl.pallas_call(attn_kernel, out_shape=(jax.ShapeDtypeStruct((64, 1024), B...  21.6 us
    ppermute x4, starting transfers between devices, shifted(): lax.ppermute(value, 'band', [(i, i + steps) for i in range(first, last)])  16.2 us
    unnamed x5, local copies, waits for them, and re-layouts  2.2 us
  transfers between devices with their start and end apart: 4, of which 0 were waited for; matrix products, arithmetic and copies ran while one was open for 3% of the time, Pallas kernels for 24%

profile of v1, /device:TPU:1, one launch (start us, length us, event | category | flops | bytes accessed | tf_op | source)
XLA Modules:
  0.0 102.8 jit_solution(6483379222719476879)
XLA Ops:
  0.6 1.0 fusion.2
  1.6 8.7 %collective-permute-start.1 = (bf16[2,64,1024]{2,1,0:T(8,128)(2,1)S(1)}, bf16[2,64,1024]{2,1,0:T(8,128)(2,1)S(1)}, u32[]{:S(2)}, u32[]{:S(2)}) collective-permute-start(bf16[2,64,1024]{2,1,0:T(8,128)(2,1)S(1)} %get-tuple-element.23), channel_id=1, source_target_pairs={{4,0},{8,4},{12,8},{16,12},{20,16},{24,20},{28,24},{32,28},{36,32}... | collective-permute-start | bytes 786440 | tf_op jit(solution)/shard_map/ppermute | solution.py:202
  10.4 1.9 %collective-permute-start = (bf16[2,64,1024]{2,1,0:T(8,128)(2,1)S(1)}, bf16[2,64,1024]{2,1,0:T(8,128)(2,1)S(1)}, u32[]{:S(2)}, u32[]{:S(2)}) collective-permute-start(bf16[2,64,1024]{2,1,0:T(8,128)(2,1)S(1)} %get-tuple-element.23), channel_id=1, source_target_pairs={{0,4},{4,8},{8,12},{12,16},{16,20},{20,24},{24,28},{28,32},{32,36}... | collective-permute-start | bytes 786440 | tf_op jit(solution)/shard_map/ppermute | solution.py:202
  12.3 0.8 subtract_select_fusion
  13.1 0.1 select_reduce_fusion
  13.2 0.6 reshape.44.inv_idx
  13.9 0.6 reshape.43.eidx
  14.5 0.7 log_multiply_fusion.bias
  15.2 29.8 %all_gather.3.grad_ref = bf16[256,1024]{1,0:T(8,128)(2,1)} all-gather(bf16[64,1024]{1,0:T(8,128)(2,1)} %param.10), channel_id=1, replica_groups=mesh['band'=128,'head'=4] {'head'}, dimensions={0}, use_global_device_ids=true | all-gather | bytes 655360 | tf_op jit(solution)/shard_map/all_gather | solution.py:223
  45.0 0.0 collective-permute-done.1
  45.0 0.0 collective-permute-done
  45.0 1.0 pad_maximum_fusion.kv_ref
  45.9 21.6 %attention_grads.1 = (bf16[64,1024]{1,0:T(8,128)(2,1)}, f32[24,128,128]{2,1,0:T(8,128)}, f32[64,256]{1,0:T(8,128)}) custom-call(s32[64]{0:T(128)} %reshape.43.eidx, s32[136]{0:T(256)} %reshape.44.inv_idx, f32[24,128]{1,0:T(8,128)} %log_multiply_fusion.bias, bf16[64,1024]{1,0:T(8,128)(2,1)} %q_ref.1, bf16[3,2,64,1024]{3,2,1,0:T(8,128)(2,1)} %pad_maximum_fusion.kv_ref, ...), custom_call_target="tpu_custom_call" | custom-call | tf_op jit(solution)/shard_map/attention_grads/pallas_call | solution.py:189
  67.5 1.5 %convert.4 = bf16[24,128,128]{2,1,0:T(8,128)(2,1)S(1)} convert(f32[24,128,128]{2,1,0:T(8,128)} %get-tuple-element.8) | non-fusion elementwise | flops 393216 | bytes 2359296 | tf_op jit(solution)/shard_map/convert.1
  69.2 2.5 %collective-permute-start.2 = (bf16[8,128,128]{2,1,0:T(8,128)(2,1)S(1)}, bf16[8,128,128]{2,1,0:T(8,128)(2,1)S(1)}, u32[]{:S(2)}, u32[]{:S(2)}) collective-permute-start(bf16[8,128,128]{2,1,0:T(8,128)(2,1)S(1)} %get-tuple-element.18), channel_id=1, source_target_pairs={{4,0},{8,4},{12,8},{16,12},{20,16},{24,20},{28,24},{32,28},{36,32}... | collective-permute-start | bytes 786440 | tf_op jit(solution)/shard_map/ppermute | solution.py:202
  71.7 3.0 %collective-permute-start.3 = (bf16[8,128,128]{2,1,0:T(8,128)(2,1)S(1)}, bf16[8,128,128]{2,1,0:T(8,128)(2,1)S(1)}, u32[]{:S(2)}, u32[]{:S(2)}) collective-permute-start(bf16[8,128,128]{2,1,0:T(8,128)(2,1)S(1)} %get-tuple-element.19), channel_id=1, source_target_pairs={{0,4},{4,8},{8,12},{12,16},{16,20},{20,24},{24,28},{28,32},{32,36}... | collective-permute-start | bytes 786440 | tf_op jit(solution)/shard_map/ppermute | solution.py:202
  74.7 24.6 %band_sum.1 = f32[64,256]{1,0:T(8,128)} custom-call(f32[64,256]{1,0:T(8,128)} %get-tuple-element.9.w_ref), custom_call_target="tpu_custom_call" | custom-call | tf_op jit(solution)/shard_map/band_sum/pallas_call | solution.py:70
  99.3 0.0 copy-start
  99.3 0.0 collective-permute-done.2
  99.3 0.0 collective-permute-done.3
  99.4 1.1 %fusion = bf16[128,8,128]{0,2,1:T(8,128)(2,1)S(1)} fusion(bf16[8,128,128]{2,1,0:T(8,128)(2,1)S(1)} %collective-permute-done.3, bf16[8,128,128]{2,1,0:T(8,128)(2,1)S(1)} %collective-permute-done.2, f32[24,128,128]{2,1,0:T(8,128)} %get-tuple-element.8), kind=kLoop, calls=%fused_computation.2 | loop fusion | flops 655360 | bytes 1310720 | tf_op jit(solution)/shard_map/transpose | solution.py:232
  100.5 0.1 fusion.4
  100.6 0.8 copy.14
  101.4 0.8 copy.13
  102.2 0.0 copy-done
  102.2 0.6 copy.16
  (2 shorter events, 0.0 us)
Async XLA Ops:
  1.6 43.3 %collective-permute-start.1 = (bf16[2,64,1024]{2,1,0:T(8,128)(2,1)S(1)}, bf16[2,64,1024]{2,1,0:T(8,128)(2,1)S(1)}, u32[]{:S(2)}, u32[]{:S(2)}) collective-permute-start(bf16[2,64,1024]{2,1,0:T(8,128)(2,1)S(1)} %get-tuple-element.23), channel_id=1, source_target_pairs={{4,0},{8,4},{12,8},{16,12},{20,16},{24,20},{28,24},{32,28},{36,32}... | collective-permute-start | bytes 786440 | tf_op jit(solution)/shard_map/ppermute | solution.py:202
  10.4 34.6 %collective-permute-start = (bf16[2,64,1024]{2,1,0:T(8,128)(2,1)S(1)}, bf16[2,64,1024]{2,1,0:T(8,128)(2,1)S(1)}, u32[]{:S(2)}, u32[]{:S(2)}) collective-permute-start(bf16[2,64,1024]{2,1,0:T(8,128)(2,1)S(1)} %get-tuple-element.23), channel_id=1, source_target_pairs={{0,4},{4,8},{8,12},{12,16},{16,20},{20,24},{24,28},{28,32},{32,36}... | collective-permute-start | bytes 786440 | tf_op jit(solution)/shard_map/ppermute | solution.py:202
  69.2 30.2 %collective-permute-start.2 = (bf16[8,128,128]{2,1,0:T(8,128)(2,1)S(1)}, bf16[8,128,128]{2,1,0:T(8,128)(2,1)S(1)}, u32[]{:S(2)}, u32[]{:S(2)}) collective-permute-start(bf16[8,128,128]{2,1,0:T(8,128)(2,1)S(1)} %get-tuple-element.18), channel_id=1, source_target_pairs={{4,0},{8,4},{12,8},{16,12},{20,16},{24,20},{28,24},{32,28},{36,32}... | collective-permute-start | bytes 786440 | tf_op jit(solution)/shard_map/ppermute | solution.py:202
  71.7 27.7 %collective-permute-start.3 = (bf16[8,128,128]{2,1,0:T(8,128)(2,1)S(1)}, bf16[8,128,128]{2,1,0:T(8,128)(2,1)S(1)}, u32[]{:S(2)}, u32[]{:S(2)}) collective-permute-start(bf16[8,128,128]{2,1,0:T(8,128)(2,1)S(1)} %get-tuple-element.19), channel_id=1, source_target_pairs={{0,4},{4,8},{8,12},{12,16},{16,20},{20,24},{24,28},{28,32},{32,36}... | collective-permute-start | bytes 786440 | tf_op jit(solution)/shard_map/ppermute | solution.py:202
  99.3 2.9 %copy-start = (f32[64,256]{1,0:T(8,128)S(1)}, f32[64,256]{1,0:T(8,128)}, u32[]{:S(2)}) copy-start(f32[64,256]{1,0:T(8,128)} %band_sum.1) | copy-start | bytes 196612

commit v2 on v1

v2 whole, which is shorter than its diff:
```python
import math
import jax
import jax.numpy as jnp
from jax import lax
from jax.experimental import pallas as pl
from jax.experimental.pallas import tpu as pltpu
from jax.sharding import PartitionSpec as P

MESH = pl.DeviceIdType.MESH
F32, BF16 = jnp.float32, jnp.bfloat16
SCALE = 32 ** -0.5
EXP2_SCALE = SCALE * math.log2(math.e)
PI_HIGH = 3.1415927410125732
PI_LOW = -8.742277657347586e-08


def dot(a, b):
    return jnp.dot(a, b, preferred_element_type=F32)


def dot_nt(a, b):
    return lax.dot_general(a, b, (((1,), (1,)), ((), ())), preferred_element_type=F32)


def head_diag(m):
    return jnp.concatenate([m[0:32, 0:128], m[32:64, 128:256]], axis=0)


def block_diag(m):
    z = jnp.zeros((32, 128), m.dtype)
    return jnp.concatenate(
        [jnp.concatenate([m[0:32], z], axis=1), jnp.concatenate([z, m[32:64]], axis=1)], axis=0
    )


def sin_to_pi(x):
    y = jnp.where(x > 0.5 * math.pi, (PI_HIGH - x) + PI_LOW, x)
    z = y * y
    r = jnp.full_like(y, 1.0 / math.factorial(13))
    for n in (11, 9, 7, 5, 3):
        r = r * z + (-1.0) ** ((n - 1) // 2) / math.factorial(n)
    return y + y * (z * r)


def prep_block(e, k, v, bias_row, kv_fm, k_tm, v_tm):
    kv_fm[e, 0:64] = k
    kv_fm[e, 64:128] = v
    high = bias_row.astype(BF16).astype(F32)
    mid = (bias_row - high).astype(BF16).astype(F32)
    low = (bias_row - high) - mid
    row = lax.broadcasted_iota(jnp.int32, (64, 128), 0)
    aug = jnp.where(row == 0, high, jnp.where(row == 1, mid, jnp.where(row == 2, low, 0.0)))
    k_tm[e] = jnp.concatenate([k, aug.astype(BF16)], axis=0).T
    v_tm[e] = jnp.concatenate([v, jnp.zeros((64, 128), BF16)], axis=0).T


def forward_block(b, q, eidx, kv_fm, k_tm, s_ref, p_ref, ps, inv_ref):
    qa = jnp.concatenate([block_diag(q), jnp.ones((64, 256), BF16)], axis=0)
    es = [eidx[b * 8 + j] for j in range(8)]
    top = None
    for j in range(8):
        s = dot(k_tm[es[j]], qa)
        s_ref[j] = s
        m8 = jnp.max(s.reshape(16, 8, 256), axis=0)
        top = m8 if top is None else jnp.maximum(top, m8)
    top = jnp.max(top, axis=0, keepdims=True) * EXP2_SCALE
    total = None
    for j in range(8):
        p = jnp.exp2(s_ref[j] * EXP2_SCALE - top)
        p_ref[b * 8 + j] = p
        l8 = jnp.sum(p.reshape(16, 8, 256), axis=0)
        total = l8 if total is None else total + l8
    inv = 1.0 / jnp.sum(total, axis=0, keepdims=True)
    inv_ref[b] = inv
    for j in range(8):
        ps[b * 8 + j, :, 256:512] = (p_ref[b * 8 + j] * inv).astype(BF16)
    v_all = jnp.concatenate([kv_fm[es[j], 64:128] for j in range(8)], axis=1)
    p_all = ps[pl.ds(b * 8, 8), :, 256:512].reshape(1024, 256)
    return head_diag(dot(v_all, p_all)).astype(BF16)


def backward_block(b, q, g, eidx, inv_idx, kv_fm, v_tm, d_ref, p_ref, ps, inv_ref, acc):
    gd = block_diag(g)
    ga = jnp.concatenate([gd, jnp.zeros((64, 256), BF16)], axis=0)
    es = [eidx[b * 8 + j] for j in range(8)]
    tot = None
    for j in range(8):
        d = dot(v_tm[es[j]], ga)
        d_ref[j] = d
        t8 = jnp.sum((p_ref[b * 8 + j] * d).reshape(16, 8, 256), axis=0)
        tot = t8 if tot is None else tot + t8
    inv = inv_ref[b]
    spread = jnp.sum(tot, axis=0, keepdims=True) * inv
    isc = inv * SCALE
    for j in range(8):
        ds = (p_ref[b * 8 + j] * isc) * (d_ref[j] - spread)
        ps[b * 8 + j, :, 0:256] = ds.astype(BF16)
    k_all = jnp.concatenate([kv_fm[es[j], 0:64] for j in range(8)], axis=1)
    d_all = ps[pl.ds(b * 8, 8), :, 0:256].reshape(1024, 256)
    dq = head_diag(dot(k_all, d_all)).astype(BF16)
    z = jnp.zeros((64, 256), BF16)
    w = jnp.concatenate(
        [jnp.concatenate([block_diag(q), z], axis=1), jnp.concatenate([z, gd], axis=1)], axis=0
    )
    for i in range(17):
        acc[b + i] += dot_nt(ps[inv_idx[b * 17 + i]], w)
    return dq


def chunk(b):
    return pl.ds(pl.multiple_of(b * 128, 128), 128)


def kernel(lists, counts, q_hbm, k_hbm, v_hbm, g_hbm, w_hbm, dq_hbm, dk_hbm, dv_hbm, dw_hbm,
           eidx, inv_idx, bias, qv, kvb, gfull, wv, kv_fm, k_tm, v_tm, s_ref, p_ref, ps, inv_ref, att, acc,
           dqv, dkv, halo_out, halo_in, pw, rc, xs, rx, mine, ry, ysum, rz, zsum, half, dwv,
           load_sem, ag_send, ag_recv, fw_send, fw_recv, kv_send, kv_recv, ho_send, ho_recv,
           c_send, c_recv, x_send, x_recv, y_send, y_recv, z_send, z_recv, a_send, a_recv, e_send, e_recv, out_sem):
    me = lax.axis_index("band")
    hi = lax.axis_index("head")
    core, x, y, z = lax.rem(me, 2), lax.rem(me // 2, 4), lax.rem(me // 8, 4), me // 32
    up, down = lax.rem(hi + 1, 4), lax.rem(hi + 3, 4)
    right, left = lax.rem(me + 1, 128), lax.rem(me + 127, 128)
    other = me + 1 - 2 * core
    x_of = [lax.rem(x + d, 4) for d in range(4)]
    xs_ids = [me + 2 * (x_of[d] - x) for d in range(4)]
    ys_ids = [me + 8 * (lax.rem(y + d, 4) - y) for d in range(4)]
    zs_ids = [me + 32 * (lax.rem(z + d, 4) - z) for d in range(4)]

    def remote(src, dst, send, recv, **to):
        return pltpu.make_async_remote_copy(src_ref=src, dst_ref=dst, send_sem=send, recv_sem=recv,
                                            device_id=to, device_id_type=MESH)

    barrier = pltpu.get_barrier_semaphore()
    for h in (up, down):
        pl.semaphore_signal(barrier, inc=1, device_id={"head": h}, device_id_type=MESH)
    for b in [left, right, other] + xs_ids[1:] + ys_ids[1:] + zs_ids[1:]:
        pl.semaphore_signal(barrier, inc=1, device_id={"band": b}, device_id_type=MESH)
    rows = pl.ds(pl.multiple_of(hi * 64, 64), 64)
    rows_below = pl.ds(pl.multiple_of(down * 64, 64), 64)
    rows_above = pl.ds(pl.multiple_of(up * 64, 64), 64)
    loads = [pltpu.make_async_copy(src, dst, load_sem.at[i]) for i, (src, dst) in enumerate([
        (g_hbm, gfull.at[rows]), (k_hbm, kvb.at[1, 0]), (v_hbm, kvb.at[1, 1]), (q_hbm, qv), (w_hbm, wv)])]
    for c in loads:
        c.start()

    def ag(c, way):
        return remote(gfull.at[rows, chunk(c)], gfull.at[rows, chunk(c)], ag_send.at[2 * c + way],
                      ag_recv.at[2 * c + way], head=(up, down)[way])

    def ag_arrived(c, way):
        src = (rows_below, rows_above)[way]
        return remote(gfull.at[src, chunk(c)], gfull.at[src, chunk(c)], ag_send.at[2 * c + way],
                      ag_recv.at[2 * c + way], head=(up, down)[way])

    rows_far = pl.ds(pl.multiple_of(lax.rem(hi + 2, 4) * 64, 64), 64)

    def fw(c):
        way = c % 2
        src = (rows_below, rows_above)[way]
        return remote(gfull.at[src, chunk(c)], gfull.at[src, chunk(c)], fw_send.at[c], fw_recv.at[c],
                      head=(up, down)[way])

    def fw_arrived(c):
        return remote(gfull.at[rows_far, chunk(c)], gfull.at[rows_far, chunk(c)], fw_send.at[c], fw_recv.at[c],
                      head=up)

    for c in loads[:3]:
        c.wait()
    pl.semaphore_wait(barrier, 14)
    for c in range(8):
        for way in range(2):
            ag(c, way).start()
    halos = [remote(kvb.at[1], kvb.at[0], kv_send.at[0], kv_recv.at[0], band=right),
             remote(kvb.at[1], kvb.at[2], kv_send.at[1], kv_recv.at[1], band=left)]
    for c in halos:
        c.start()

    first = me * 8 - 8

    def table(b, _):
        count = counts[b]
        es = []
        for j in range(8):
            e = jnp.where(j < count, lists[b, j] - first, 24)
            eidx[b * 8 + j] = e
            es.append(e)
        for i in range(17):
            t = jnp.int32(64)
            for j in range(8):
                t = jnp.where(es[j] == b + i, b * 8 + j, t)
            inv_idx[b * 17 + i] = t
        return 0
    lax.fori_loop(0, 8, table, 0)
    shape = (24, 128)
    pos = (first + lax.broadcasted_iota(jnp.int32, shape, 0)) * 128 + lax.broadcasted_iota(jnp.int32, shape, 1)
    pos = jnp.clip(pos, 0, 131071).astype(F32)
    bias[...] = jnp.log(sin_to_pi(math.pi * (pos + 0.5) / 131072)) * (32 ** 0.5)

    def prep(side):
        def one(i, _):
            e = side * 8 + i
            prep_block(e, kvb[side, 0, :, chunk(i)], kvb[side, 1, :, chunk(i)], bias[pl.ds(e, 1), :],
                       kv_fm, k_tm, v_tm)
            return 0
        lax.fori_loop(0, 8, one, 0)

    zero = jnp.zeros((64, 128), BF16)
    prep_block(24, zero, zero, jnp.full((1, 128), -1e30, F32), kv_fm, k_tm, v_tm)
    ps[64] = jnp.zeros((128, 512), BF16)
    acc[...] = jnp.zeros_like(acc)
    prep(1)
    halos[0].wait_recv()
    prep(0)
    halos[1].wait_recv()
    prep(2)
    loads[3].wait()
    loads[4].wait()

    def forward_chunk(c):
        ag_arrived(c, c % 2).wait_recv()
        fw(c).start()

    def fwd(b, _):
        att[:, chunk(b)] = forward_block(b, qv[:, chunk(b)], eidx, kv_fm, k_tm, s_ref, p_ref, ps, inv_ref)
        for at, cs in FORWARD_AT.items():
            @pl.when(b == at)
            def _():
                for c in cs:
                    forward_chunk(c)
        return 0
    lax.fori_loop(0, 8, fwd, 0)

    keep, give = core, 1 - core
    core_copy = remote(pw.at[give], rc, c_send.at[0], c_recv.at[0], band=other)
    x_copies = [remote(xs.at[x_of[d]], rx.at[d], x_send.at[d], x_recv.at[d], band=xs_ids[d]) for d in range(1, 4)]
    y_copies = [remote(mine, ry.at[d], y_send.at[d], y_recv.at[d], band=ys_ids[d]) for d in range(1, 4)]
    z_copies = [remote(ysum, rz.at[d], z_send.at[d], z_recv.at[d], band=zs_ids[d]) for d in range(1, 4)]
    a_copies = [remote(zsum, half.at[x], a_send.at[d], a_recv.at[d], band=xs_ids[d]) for d in range(1, 4)]
    a_waits = [remote(zsum, half.at[x_of[d]], a_send.at[d], a_recv.at[d], band=xs_ids[d]) for d in range(1, 4)]
    e_copy = remote(half, dwv.at[core], e_send.at[0], e_recv.at[0], band=other)
    e_wait = remote(half, dwv.at[give], e_send.at[0], e_recv.at[0], band=other)

    def sum_core():
        total = dot_nt(att[...], gfull[...])
        pw[0] = total[:, 0:128]
        pw[1] = total[:, 128:256]
        core_copy.start()

    def sum_x():
        core_copy.wait_recv()
        xs[...] = (pw[keep] + rc[...]).reshape(4, 16, 128)
        for c in x_copies:
            c.start()

    def sum_y():
        for c in x_copies:
            c.wait_recv()
        mine[...] = xs[x] + rx[1] + rx[2] + rx[3]
        for c in y_copies:
            c.start()

    def sum_z():
        for c in y_copies:
            c.wait_recv()
        ysum[...] = mine[...] + ry[1] + ry[2] + ry[3]
        for c in z_copies:
            c.start()

    def gather_x():
        for c in z_copies:
            c.wait_recv()
        t = ysum[...] + rz[1] + rz[2] + rz[3]
        zsum[...] = t
        half[x] = t
        for c in a_copies:
            c.start()

    def gather_core():
        for c in a_waits:
            c.wait_recv()
        e_copy.start()
        dwv[core] = half[...]

    def rest_of_chunk(c):
        ag_arrived(c, 1 - c % 2).wait_recv()
        fw_arrived(c).wait_recv()

    halo_copies = [remote(halo_out.at[0], halo_in.at[0], ho_send.at[0], ho_recv.at[0], band=left),
                   remote(halo_out.at[1], halo_in.at[1], ho_send.at[1], ho_recv.at[1], band=right)]

    def bwd(b, _):
        for at, cs in WAIT_AT.items():
            @pl.when(b == at)
            def _():
                for kind, c in cs:
                    (forward_chunk if kind else rest_of_chunk)(c)
        for at, step in SUM_AT.items():
            @pl.when(b == at)
            def _():
                {"core": sum_core, "x": sum_x, "y": sum_y, "z": sum_z}[step]()
        g = dot(wv[...], gfull[:, chunk(b)]).astype(BF16)
        dqv[:, chunk(b)] = backward_block(b, qv[:, chunk(b)], g, eidx, inv_idx, kv_fm, v_tm, s_ref, p_ref, ps,
                                          inv_ref, acc)
        return 0
    lax.fori_loop(0, 8, bwd, 0)
    outs = [pltpu.make_async_copy(dqv, dq_hbm, out_sem.at[0])]
    outs[0].start()
    halo_out[0] = acc[0:8].astype(BF16)
    halo_copies[0].start()
    halo_out[1] = acc[16:24].astype(BF16)
    halo_copies[1].start()
    for step in ("core", "x", "y", "z"):
        if step not in SUM_AT.values():
            {"core": sum_core, "x": sum_x, "y": sum_y, "z": sum_z}[step]()
    gather_x()
    for c in halo_copies:
        c.wait_recv()

    def finish(i, _):
        t = acc[8 + i] + halo_in[0, i].astype(F32) + halo_in[1, i].astype(F32)
        dkv[:, chunk(i)] = t.T.astype(BF16)
        return 0
    lax.fori_loop(0, 8, finish, 0)
    outs.append(pltpu.make_async_copy(dkv.at[0:64], dk_hbm, out_sem.at[1]))
    outs.append(pltpu.make_async_copy(dkv.at[64:128], dv_hbm, out_sem.at[2]))
    outs[1].start()
    outs[2].start()
    gather_core()
    e_wait.wait_recv()
    for i in range(2):
        c = pltpu.make_async_copy(dwv.at[i], dw_hbm.at[i], out_sem.at[3 + i])
        c.start()
        outs.append(c)
    for c in range(8):
        for way in range(2):
            ag(c, way).wait_send()
        fw(c).wait_send()
    for c in halos + halo_copies + [core_copy] + x_copies + y_copies + z_copies + a_copies + [e_copy]:
        c.wait_send()
    for c in outs:
        c.wait()


FORWARD_AT = {0: (0, 1), 2: (2,), 4: (3,), 6: (4,), 7: (5,)}
WAIT_AT = {0: ((1, 6), (0, 0)), 1: ((1, 7), (0, 1)), 2: ((0, 2),), 3: ((0, 3),),
           4: ((0, 4), (0, 5), (0, 6), (0, 7))}
SUM_AT = {4: "core", 5: "x", 7: "y"}


def shards(queries, keys, values, grad_out, w_out, key_lists, key_counts):
    V, S, D = pltpu.VMEM, pltpu.SMEM, pltpu.SemaphoreType.DMA
    hbm = pl.BlockSpec(memory_space=pl.ANY)
    smem = pl.BlockSpec(memory_space=S)
    slab = jax.ShapeDtypeStruct((64, 1024), BF16)
    piece = V((16, 128), F32)
    pieces = V((4, 16, 128), F32)
    dq, dk, dv, dw = pl.pallas_call(
        kernel,
        out_shape=(slab, slab, slab, jax.ShapeDtypeStruct((2, 4, 16, 128), F32)),
        in_specs=[smem, smem] + [hbm] * 5,
        out_specs=[hbm] * 4,
        scratch_shapes=[
            S((64,), jnp.int32), S((136,), jnp.int32), V((24, 128), F32), V((64, 1024), BF16),
            V((3, 2, 64, 1024), BF16), V((256, 1024), BF16), V((64, 256), BF16),
            V((25, 128, 128), BF16), V((25, 128, 128), BF16), V((25, 128, 128), BF16),
            V((8, 128, 256), F32), V((64, 128, 256), F32), V((65, 128, 512), BF16), V((8, 1, 256), F32),
            V((64, 1024), BF16), V((24, 128, 128), F32), V((64, 1024), BF16), V((128, 1024), BF16),
            V((2, 8, 128, 128), BF16), V((2, 8, 128, 128), BF16),
            V((2, 64, 128), F32), V((64, 128), F32), pieces, pieces, piece, pieces, piece, pieces, piece, pieces,
            V((2, 4, 16, 128), F32),
            D((5,)), D((16,)), D((16,)), D((8,)), D((8,)), D((2,)), D((2,)), D((2,)), D((2,)),
            D((1,)), D((1,)), D((4,)), D((4,)), D((4,)), D((4,)), D((4,)), D((4,)), D((4,)), D((4,)),
            D((1,)), D((1,)), D((5,)),
        ],
        compiler_params=pltpu.CompilerParams(collective_id=0, has_side_effects=True, vmem_limit_bytes=60 * 2**20),
        name="attention_grads",
    )(key_lists, key_counts, queries, keys, values, grad_out, w_out)
    dw = jnp.concatenate([dw[0].reshape(64, 128), dw[1].reshape(64, 128)], axis=1)
    return dq, dk, dv, dw


def solution(mesh):
    split = P("head", "band")
    in_specs = (split, split, split, split, P("head", None), P("band", None), P("band"))
    out_specs = (split, split, split, P("head", None))
    return jax.shard_map(shards, mesh=mesh, in_specs=in_specs, out_specs=out_specs, check_vma=False)
```

time: 103 us -> 72.7 us (0.71)
  blocking collectives: 29.8 us -> 0 us
  Pallas kernels: 46.2 us -> 67.4 us
  starting transfers between devices: 16.2 us -> 0 us
  other arithmetic: 6.2 us -> 0.63 us
    all_gather x1 -> x0, blocking collectives: 29.8 us -> none  [shards(): full_grad = lax.all_gather(grad_out, 'head', axis=0, tiled=True)]
    pallas_call x2 -> x1, Pallas kernels: 46.2 us -> 67.4 us  [shards(): pl.pallas_call(kernel, out_shape=(slab, slab, slab, jax.ShapeDtypeStruct(...]
    ppermute x4 -> x0, starting transfers between devices: 16.2 us -> none  [shifted(): lax.ppermute(value, 'band', [(i, i + steps) for i in range(first, last)])]
    another operation x3 -> x0, other arithmetic: 3.52 us -> none  [the longest x2 1.98 us: shards(): kv = jnp.stack([shifted(pair, 1), pair, shifted(pair, -1)])]
    reshape x2 -> x0, local copies, waits for them, and re-layouts: 1.29 us -> none  [tables(): return (eidx.reshape(-1), inv_idx.reshape(-1), bias)]
    transpose x1 -> x0, other arithmetic: 1.13 us -> none  [shards(): both = own.transpose(2, 0, 1).reshape(128, 1024)]
    unnamed x5 -> x9, local copies, waits for them, and re-layouts: 2.2 us -> 2.56 us
  transfers between devices with their start and end apart: 4 -> 0, of which waited for: 0 -> 0; matrix products, arithmetic and copies ran while one was open for 3% -> 0% of each run, Pallas kernels for 24% -> 0%
where the time goes in v2:
time: 72.7 us; the launch traced here: 72.1 us
  Pallas kernels  67.4 us (93%)
  local copies, waits for them, and re-layouts  3.38 us (5%)
    pallas_call x1, Pallas kernels, shards(): pl.pallas_call(kernel, out_shape=(slab, slab, slab, jax.ShapeDtypeStruct(...  67.4 us
    unnamed x9, local copies, waits for them, and re-layouts  2.56 us

profile of v2, /device:TPU:1, one launch (start us, length us, event | category | flops | bytes accessed | tf_op | source)
XLA Modules:
  0.0 72.1 jit_solution(3980113727034264110)
XLA Ops:
  0.6 67.4 %attention_grads.1 = (bf16[64,1024]{1,0:T(8,128)(2,1)}, bf16[64,1024]{1,0:T(8,128)(2,1)}, bf16[64,1024]{1,0:T(8,128)(2,1)}, f32[2,4,16,128]{3,2,1,0:T(8,128)}) custom-call(s32[8,8]{1,0:T(8,128)} %lists.1, s32[8]{0:T(128)} %counts.1, bf16[64,1024]{1,0:T(8,128)(2,1)} %q_hbm.1, bf16[64,1024]{1,0:T(8,128)(2,1)} %k_hbm.1, bf16[64,1024]{1,0:T(8,128)(2,1)} %v_hbm.1, ...), custom_call_target="tpu_custom_call" | custom-call | tf_op jit(solution)/shard_map/attention_grads/pallas_call | solution.py:358
  68.0 0.0 copy-start.2
  68.1 0.8 %fusion = (f32[1,4,16,128]{3,2,1,0:T(8,128)S(1)}, f32[1,4,16,128]{3,2,1,0:T(8,128)S(1)}) fusion(f32[2,4,16,128]{3,2,1,0:T(8,128)} %get-tuple-element.11), kind=kLoop, calls=%fused_computation.1 | loop fusion | bytes 131072 | tf_op jit(solution)/shard_map/slice | solution.py:379
  68.9 0.6 pad_maximum_fusion
  69.5 0.0 copy-done.2
  69.5 0.0 copy-start.1
  69.5 0.7 copy.14
  70.2 0.3 copy-done.1
  70.5 0.0 copy-start
  70.5 0.7 copy.15
  71.1 0.3 copy-done
  71.4 0.7 copy.16
Async XLA Ops:
  68.0 1.5 %copy-start.2 = (bf16[64,1024]{1,0:T(8,128)(2,1)S(1)}, bf16[64,1024]{1,0:T(8,128)(2,1)}, u32[]{:S(2)}) copy-start(bf16[64,1024]{1,0:T(8,128)(2,1)} %get-tuple-element.18) | copy-start | bytes 393220
  69.5 1.0 %copy-start.1 = (bf16[64,1024]{1,0:T(8,128)(2,1)S(1)}, bf16[64,1024]{1,0:T(8,128)(2,1)}, u32[]{:S(2)}) copy-start(bf16[64,1024]{1,0:T(8,128)(2,1)} %get-tuple-element.19) | copy-start | bytes 393220
  70.5 1.0 %copy-start = (bf16[64,1024]{1,0:T(8,128)(2,1)S(1)}, bf16[64,1024]{1,0:T(8,128)(2,1)}, u32[]{:S(2)}) copy-start(bf16[64,1024]{1,0:T(8,128)(2,1)} %get-tuple-element.20) | copy-start | bytes 393220

commit v3 on v2

--- a/solution.py
+++ b/solution.py
@@ -42,15 +42,18 @@
     return y + y * (z * r)
 
 
-def prep_block(e, k, v, bias_row, kv_fm, k_tm, v_tm):
+def prep_keys(e, k, bias_row, kv_fm, k_tm):
     kv_fm[e, 0:64] = k
-    kv_fm[e, 64:128] = v
     high = bias_row.astype(BF16).astype(F32)
     mid = (bias_row - high).astype(BF16).astype(F32)
     low = (bias_row - high) - mid
     row = lax.broadcasted_iota(jnp.int32, (64, 128), 0)
     aug = jnp.where(row == 0, high, jnp.where(row == 1, mid, jnp.where(row == 2, low, 0.0)))
     k_tm[e] = jnp.concatenate([k, aug.astype(BF16)], axis=0).T
+
+
+def prep_values(e, v, kv_fm, v_tm):
+    kv_fm[e, 64:128] = v
     v_tm[e] = jnp.concatenate([v, jnp.zeros((64, 128), BF16)], axis=0).T
 
 
@@ -74,12 +77,15 @@
     inv_ref[b] = inv
     for j in range(8):
         ps[b * 8 + j, :, 256:512] = (p_ref[b * 8 + j] * inv).astype(BF16)
-    v_all = jnp.concatenate([kv_fm[es[j], 64:128] for j in range(8)], axis=1)
+
+
+def attended_block(b, eidx, kv_fm, ps):
+    v_all = jnp.concatenate([kv_fm[eidx[b * 8 + j], 64:128] for j in range(8)], axis=1)
     p_all = ps[pl.ds(b * 8, 8), :, 256:512].reshape(1024, 256)
     return head_diag(dot(v_all, p_all)).astype(BF16)
 
 
-def backward_block(b, q, g, eidx, inv_idx, kv_fm, v_tm, d_ref, p_ref, ps, inv_ref, acc):
+def backward_block(b, q, g, eidx, inv_idx, kv_fm, v_tm, d_ref, p_ref, ps, inv_ref, acc, tmp, middle):
     gd = block_diag(g)
     ga = jnp.concatenate([gd, jnp.zeros((64, 256), BF16)], axis=0)
     es = [eidx[b * 8 + j] for j in range(8)]
@@ -102,8 +108,10 @@
     w = jnp.concatenate(
         [jnp.concatenate([block_diag(q), z], axis=1), jnp.concatenate([z, gd], axis=1)], axis=0
     )
+    middle()
+    tmp[0:8] = dot(ps[pl.ds(b * 8, 8)].reshape(1024, 512), w.T).reshape(8, 128, 128)
     for i in range(17):
-        acc[b + i] += dot_nt(ps[inv_idx[b * 17 + i]], w)
+        acc[b + i] += tmp[inv_idx[b * 17 + i]]
     return dq
 
 
@@ -111,11 +119,11 @@
     return pl.ds(pl.multiple_of(b * 128, 128), 128)
 
 
-def kernel(lists, counts, q_hbm, k_hbm, v_hbm, g_hbm, w_hbm, dq_hbm, dk_hbm, dv_hbm, dw_hbm,
-           eidx, inv_idx, bias, qv, kvb, gfull, wv, kv_fm, k_tm, v_tm, s_ref, p_ref, ps, inv_ref, att, acc,
+def kernel(lists, counts, q_hbm, k_hbm, v_hbm, g_hbm, w_hbm, grads_hbm, dw_hbm,
+           eidx, inv_idx, bias, qv, kvb, gfull, wv, kv_fm, k_tm, v_tm, s_ref, p_ref, ps, inv_ref, att, acc, tmp,
            dqv, dkv, halo_out, halo_in, pw, rc, xs, rx, mine, ry, ysum, rz, zsum, half, dwv,
            load_sem, ag_send, ag_recv, fw_send, fw_recv, kv_send, kv_recv, ho_send, ho_recv,
-           c_send, c_recv, x_send, x_recv, y_send, y_recv, z_send, z_recv, a_send, a_recv, e_send, e_recv, out_sem):
+           c_send, c_recv, x_send, x_recv, y_send, y_recv, z_send, z_recv, a_send, a_recv, e_send, e_recv, out_sem, go):
     me = lax.axis_index("band")
     hi = lax.axis_index("head")
     core, x, y, z = lax.rem(me, 2), lax.rem(me // 2, 4), lax.rem(me // 8, 4), me // 32
@@ -137,44 +145,37 @@
     for b in [left, right, other] + xs_ids[1:] + ys_ids[1:] + zs_ids[1:]:
         pl.semaphore_signal(barrier, inc=1, device_id={"band": b}, device_id_type=MESH)
     rows = pl.ds(pl.multiple_of(hi * 64, 64), 64)
-    rows_below = pl.ds(pl.multiple_of(down * 64, 64), 64)
-    rows_above = pl.ds(pl.multiple_of(up * 64, 64), 64)
     loads = [pltpu.make_async_copy(src, dst, load_sem.at[i]) for i, (src, dst) in enumerate([
-        (g_hbm, gfull.at[rows]), (k_hbm, kvb.at[1, 0]), (v_hbm, kvb.at[1, 1]), (q_hbm, qv), (w_hbm, wv)])]
+        (k_hbm, kvb.at[1, 0]), (v_hbm, kvb.at[1, 1]), (q_hbm, qv), (w_hbm, wv), (g_hbm, gfull.at[rows])])]
     for c in loads:
         c.start()
 
+    column_low, column_high = x + y == 0, x + y == 6
+
     def ag(c, way):
-        return remote(gfull.at[rows, chunk(c)], gfull.at[rows, chunk(c)], ag_send.at[2 * c + way],
+        return remote(g_hbm.at[:, chunk(c)], gfull.at[rows, chunk(c)], ag_send.at[2 * c + way],
                       ag_recv.at[2 * c + way], head=(up, down)[way])
 
-    def ag_arrived(c, way):
-        src = (rows_below, rows_above)[way]
-        return remote(gfull.at[src, chunk(c)], gfull.at[src, chunk(c)], ag_send.at[2 * c + way],
-                      ag_recv.at[2 * c + way], head=(up, down)[way])
-
     rows_far = pl.ds(pl.multiple_of(lax.rem(hi + 2, 4) * 64, 64), 64)
 
+    def way_of(c):
+        far_low, far_high = (0, 1)
+        way = lax.rem(c, 2)
+        way = jnp.where(jnp.logical_and(column_low, c == 7), far_low, way)
+        return jnp.where(jnp.logical_and(column_high, c == 6), far_high, way)
+
+    def rows_from(way):
+        return pl.ds(pl.multiple_of(jnp.where(way == 0, down, up) * 64, 64), 64)
+
     def fw(c):
-        way = c % 2
-        src = (rows_below, rows_above)[way]
+        way = way_of(c)
+        src = rows_from(way)
         return remote(gfull.at[src, chunk(c)], gfull.at[src, chunk(c)], fw_send.at[c], fw_recv.at[c],
-                      head=(up, down)[way])
+                      head=jnp.where(way == 0, up, down))
 
     def fw_arrived(c):
         return remote(gfull.at[rows_far, chunk(c)], gfull.at[rows_far, chunk(c)], fw_send.at[c], fw_recv.at[c],
                       head=up)
-
-    for c in loads[:3]:
-        c.wait()
-    pl.semaphore_wait(barrier, 14)
-    for c in range(8):
-        for way in range(2):
-            ag(c, way).start()
-    halos = [remote(kvb.at[1], kvb.at[0], kv_send.at[0], kv_recv.at[0], band=right),
-             remote(kvb.at[1], kvb.at[2], kv_send.at[1], kv_recv.at[1], band=left)]
-    for c in halos:
-        c.start()
 
     first = me * 8 - 8
 
@@ -186,9 +187,9 @@
             eidx[b * 8 + j] = e
             es.append(e)
         for i in range(17):
-            t = jnp.int32(64)
+            t = jnp.int32(8)
             for j in range(8):
-                t = jnp.where(es[j] == b + i, b * 8 + j, t)
+                t = jnp.where(es[j] == b + i, j, t)
             inv_idx[b * 17 + i] = t
         return 0
     lax.fori_loop(0, 8, table, 0)
@@ -197,39 +198,115 @@
     pos = jnp.clip(pos, 0, 131071).astype(F32)
     bias[...] = jnp.log(sin_to_pi(math.pi * (pos + 0.5) / 131072)) * (32 ** 0.5)
 
-    def prep(side):
+    has_left, has_right = me > 0, me < 127
+
+    def halo(side, i):
+        return remote((k_hbm, v_hbm)[i], kvb.at[side, i], kv_send.at[side + i], kv_recv.at[side + i],
+                      band=right if side == 0 else left)
+
+    pl.semaphore_wait(barrier, 14)
+
+    @pl.when(has_right)
+    def _():
+        for i in range(2):
+            halo(0, i).start()
+
+    @pl.when(has_left)
+    def _():
+        for i in range(2):
+            halo(2, i).start()
+
+    def start_gather(ways):
+        for c in range(8):
+            for way in ways:
+                ag(c, way).start()
+
+    column = jnp.logical_or(x + y == 0, x + y == 6)
+    paired = jnp.logical_and(column, jnp.where(x == 0, z > 0, z < 3))
+    crossing = jnp.logical_and(paired, core == jnp.where(x == 0, 0, 1))
+    cross_low = jnp.logical_and(crossing, core == 0)
+    cross_high = jnp.logical_and(crossing, core == 1)
+    pl.when(jnp.logical_not(column))(lambda: start_gather((0, 1)))
+    pl.when(column_low)(lambda: start_gather((0,)))
+    pl.when(column_high)(lambda: start_gather((1,)))
+
+    def keys_of(side):
         def one(i, _):
             e = side * 8 + i
-            prep_block(e, kvb[side, 0, :, chunk(i)], kvb[side, 1, :, chunk(i)], bias[pl.ds(e, 1), :],
-                       kv_fm, k_tm, v_tm)
+            prep_keys(e, kvb[side, 0, :, chunk(i)], bias[pl.ds(e, 1), :], kv_fm, k_tm)
             return 0
         lax.fori_loop(0, 8, one, 0)
 
+    def values_of(side):
+        def one(i, _):
+            prep_values(side * 8 + i, kvb[side, 1, :, chunk(i)], kv_fm, v_tm)
+            return 0
+        lax.fori_loop(0, 8, one, 0)
+
     zero = jnp.zeros((64, 128), BF16)
-    prep_block(24, zero, zero, jnp.full((1, 128), -1e30, F32), kv_fm, k_tm, v_tm)
-    ps[64] = jnp.zeros((128, 512), BF16)
+    prep_keys(24, zero, jnp.full((1, 128), -1e30, F32), kv_fm, k_tm)
+    prep_values(24, zero, kv_fm, v_tm)
+    tmp[8] = jnp.zeros((128, 128), F32)
     acc[...] = jnp.zeros_like(acc)
-    prep(1)
-    halos[0].wait_recv()
-    prep(0)
-    halos[1].wait_recv()
-    prep(2)
-    loads[3].wait()
-    loads[4].wait()
+    for i in range(4):
+        loads[i].wait()
+    keys_of(1)
+    values_of(1)
+
+    pl.when(cross_low)(lambda: halo(2, 0).wait_send())
+    pl.when(cross_high)(lambda: halo(0, 0).wait_send())
+
+    @pl.when(crossing)
+    def _():
+        pl.semaphore_signal(go, inc=1, device_id={"band": other}, device_id_type=MESH)
+
+    @pl.when(jnp.logical_and(paired, jnp.logical_not(crossing)))
+    def _():
+        pl.semaphore_wait(go, 1)
+    pl.when(column_low)(lambda: start_gather((1,)))
+    pl.when(column_high)(lambda: start_gather((0,)))
+
+    def arrived(side, i, prep):
+        halo(side, i).wait_recv()
+        prep(side)
+    pl.when(has_left)(lambda: arrived(0, 0, keys_of))
+    pl.when(has_right)(lambda: arrived(2, 0, keys_of))
+
+    def ag_arrived(c, way):
+        src = rows_from(way)
+        return remote(gfull.at[src, chunk(c)], gfull.at[src, chunk(c)], ag_send.at[2 * c + way],
+                      ag_recv.at[2 * c + way], head=jnp.where(way == 0, up, down))
 
     def forward_chunk(c):
-        ag_arrived(c, c % 2).wait_recv()
+        ag_arrived(c, way_of(c)).wait_recv()
         fw(c).start()
 
     def fwd(b, _):
-        att[:, chunk(b)] = forward_block(b, qv[:, chunk(b)], eidx, kv_fm, k_tm, s_ref, p_ref, ps, inv_ref)
+        forward_block(b, qv[:, chunk(b)], eidx, kv_fm, k_tm, s_ref, p_ref, ps, inv_ref)
         for at, cs in FORWARD_AT.items():
-            @pl.when(b == at)
+            @pl.when(jnp.logical_and(b == at, jnp.logical_not(column)))
             def _():
                 for c in cs:
                     forward_chunk(c)
         return 0
     lax.fori_loop(0, 8, fwd, 0)
+    pl.when(has_left)(lambda: arrived(0, 1, values_of))
+    pl.when(has_right)(lambda: arrived(2, 1, values_of))
+
+    def attend(b, _):
+        att[:, chunk(b)] = attended_block(b, eidx, kv_fm, ps)
+        return 0
+    lax.fori_loop(0, 8, attend, 0)
+
+    @pl.when(column)
+    def _():
+        for c in range(8):
+            forward_chunk(c)
+
+    @pl.when(jnp.logical_not(column))
+    def _():
+        for c in FORWARD_LAST:
+            forward_chunk(c)
 
     keep, give = core, 1 - core
     core_copy = remote(pw.at[give], rc, c_send.at[0], c_recv.at[0], band=other)
@@ -283,69 +360,112 @@
         dwv[core] = half[...]
 
     def rest_of_chunk(c):
-        ag_arrived(c, 1 - c % 2).wait_recv()
+        ag_arrived(c, 1 - way_of(c)).wait_recv()
         fw_arrived(c).wait_recv()
 
-    halo_copies = [remote(halo_out.at[0], halo_in.at[0], ho_send.at[0], ho_recv.at[0], band=left),
-                   remote(halo_out.at[1], halo_in.at[1], ho_send.at[1], ho_recv.at[1], band=right)]
+    start = jnp.where(column, START_LATE, START)
+
+    def halo_back(side, i):
+        return remote(halo_out.at[side, i], halo_in.at[side, i], ho_send.at[side * 8 + i], ho_recv.at[side * 8 + i],
+                      band=(left, right)[side])
+
+    steps = {"core": sum_core, "x": sum_x, "y": sum_y, "z": sum_z}
 
     def bwd(b, _):
-        for at, cs in WAIT_AT.items():
-            @pl.when(b == at)
-            def _():
-                for kind, c in cs:
-                    (forward_chunk if kind else rest_of_chunk)(c)
-        for at, step in SUM_AT.items():
-            @pl.when(b == at)
-            def _():
-                {"core": sum_core, "x": sum_x, "y": sum_y, "z": sum_z}[step]()
+        pl.when(b < start)(lambda: rest_of_chunk(b))
+
+        @pl.when(b == start)
+        def _():
+            pl.loop(b, 8)(rest_of_chunk)
+
+        def serve(mid):
+            for at, step in SUM_AT.items():
+                if at % 2 == mid:
+                    pl.when(b == start + at // 2)(steps[step])
+        serve(0)
         g = dot(wv[...], gfull[:, chunk(b)]).astype(BF16)
         dqv[:, chunk(b)] = backward_block(b, qv[:, chunk(b)], g, eidx, inv_idx, kv_fm, v_tm, s_ref, p_ref, ps,
-                                          inv_ref, acc)
+                                          inv_ref, acc, tmp, lambda: serve(1))
+        @pl.when(has_left)
+        def _():
+            halo_out[0, b] = acc[b].astype(BF16)
+            halo_back(0, b).start()
         return 0
+    loads[4].wait()
     lax.fori_loop(0, 8, bwd, 0)
-    outs = [pltpu.make_async_copy(dqv, dq_hbm, out_sem.at[0])]
+
+    def send_upper(i, _):
+        halo_out[1, i] = acc[16 + i].astype(BF16)
+        halo_back(1, i).start()
+        return 0
+
+    @pl.when(has_right)
+    def _():
+        lax.fori_loop(0, 8, send_upper, 0)
+    outs = [pltpu.make_async_copy(dqv, grads_hbm.at[0], out_sem.at[0])]
     outs[0].start()
-    halo_out[0] = acc[0:8].astype(BF16)
-    halo_copies[0].start()
-    halo_out[1] = acc[16:24].astype(BF16)
-    halo_copies[1].start()
     for step in ("core", "x", "y", "z"):
         if step not in SUM_AT.values():
-            {"core": sum_core, "x": sum_x, "y": sum_y, "z": sum_z}[step]()
+            steps[step]()
     gather_x()
-    for c in halo_copies:
-        c.wait_recv()
+
+    @pl.when(jnp.logical_not(has_right))
+    def _():
+        halo_in[0] = jnp.zeros((8, 128, 128), BF16)
+
+    @pl.when(jnp.logical_not(has_left))
+    def _():
+        halo_in[1] = jnp.zeros((8, 128, 128), BF16)
 
     def finish(i, _):
+        pl.when(has_right)(lambda: halo_back(0, i).wait_recv())
+        pl.when(has_left)(lambda: halo_back(1, i).wait_recv())
         t = acc[8 + i] + halo_in[0, i].astype(F32) + halo_in[1, i].astype(F32)
         dkv[:, chunk(i)] = t.T.astype(BF16)
         return 0
     lax.fori_loop(0, 8, finish, 0)
-    outs.append(pltpu.make_async_copy(dkv.at[0:64], dk_hbm, out_sem.at[1]))
-    outs.append(pltpu.make_async_copy(dkv.at[64:128], dv_hbm, out_sem.at[2]))
+    outs.append(pltpu.make_async_copy(dkv.at[0:64], grads_hbm.at[1], out_sem.at[1]))
+    outs.append(pltpu.make_async_copy(dkv.at[64:128], grads_hbm.at[2], out_sem.at[2]))
     outs[1].start()
     outs[2].start()
     gather_core()
     e_wait.wait_recv()
     for i in range(2):
-        c = pltpu.make_async_copy(dwv.at[i], dw_hbm.at[i], out_sem.at[3 + i])
-        c.start()
-        outs.append(c)
+        for r in range(4):
+            c = pltpu.make_async_copy(dwv.at[i, r], dw_hbm.at[r * 16:r * 16 + 16, i * 128:i * 128 + 128], out_sem.at[3 + i * 4 + r])
+            c.start()
+            outs.append(c)
     for c in range(8):
         for way in range(2):
             ag(c, way).wait_send()
         fw(c).wait_send()
-    for c in halos + halo_copies + [core_copy] + x_copies + y_copies + z_copies + a_copies + [e_copy]:
+
+    @pl.when(has_left)
+    def _():
+        for c in range(8):
+            halo_back(0, c).wait_send()
+
+    pl.when(jnp.logical_and(has_left, jnp.logical_not(cross_low)))(lambda: halo(2, 0).wait_send())
+    pl.when(has_left)(lambda: halo(2, 1).wait_send())
+
+    @pl.when(has_right)
+    def _():
+        for c in range(8):
+            halo_back(1, c).wait_send()
+
+    pl.when(jnp.logical_and(has_right, jnp.logical_not(cross_high)))(lambda: halo(0, 0).wait_send())
+    pl.when(has_right)(lambda: halo(0, 1).wait_send())
+
+    for c in [core_copy] + x_copies + y_copies + z_copies + a_copies + [e_copy]:
         c.wait_send()
     for c in outs:
         c.wait()
 
 
-FORWARD_AT = {0: (0, 1), 2: (2,), 4: (3,), 6: (4,), 7: (5,)}
-WAIT_AT = {0: ((1, 6), (0, 0)), 1: ((1, 7), (0, 1)), 2: ((0, 2),), 3: ((0, 3),),
-           4: ((0, 4), (0, 5), (0, 6), (0, 7))}
-SUM_AT = {4: "core", 5: "x", 7: "y"}
+FORWARD_AT = {3: (0,), 5: (1,), 7: (2, 3)}
+FORWARD_LAST = (4, 5, 6, 7)
+START, START_LATE = 3, 3
+SUM_AT = {0: "core", 2: "x", 6: "y"}
 
 
 def shards(queries, keys, values, grad_out, w_out, key_lists, key_counts):
@@ -355,29 +475,28 @@
     slab = jax.ShapeDtypeStruct((64, 1024), BF16)
     piece = V((16, 128), F32)
     pieces = V((4, 16, 128), F32)
-    dq, dk, dv, dw = pl.pallas_call(
+    grads, dw = pl.pallas_call(
         kernel,
-        out_shape=(slab, slab, slab, jax.ShapeDtypeStruct((2, 4, 16, 128), F32)),
+        out_shape=(jax.ShapeDtypeStruct((3, 64, 1024), BF16), jax.ShapeDtypeStruct((64, 256), F32)),
         in_specs=[smem, smem] + [hbm] * 5,
-        out_specs=[hbm] * 4,
+        out_specs=[hbm] * 2,
         scratch_shapes=[
             S((64,), jnp.int32), S((136,), jnp.int32), V((24, 128), F32), V((64, 1024), BF16),
             V((3, 2, 64, 1024), BF16), V((256, 1024), BF16), V((64, 256), BF16),
             V((25, 128, 128), BF16), V((25, 128, 128), BF16), V((25, 128, 128), BF16),
-            V((8, 128, 256), F32), V((64, 128, 256), F32), V((65, 128, 512), BF16), V((8, 1, 256), F32),
-            V((64, 1024), BF16), V((24, 128, 128), F32), V((64, 1024), BF16), V((128, 1024), BF16),
+            V((8, 128, 256), F32), V((64, 128, 256), F32), V((64, 128, 512), BF16), V((8, 1, 256), F32),
+            V((64, 1024), BF16), V((24, 128, 128), F32), V((9, 128, 128), F32), V((64, 1024), BF16), V((128, 1024), BF16),
             V((2, 8, 128, 128), BF16), V((2, 8, 128, 128), BF16),
             V((2, 64, 128), F32), V((64, 128), F32), pieces, pieces, piece, pieces, piece, pieces, piece, pieces,
             V((2, 4, 16, 128), F32),
-            D((5,)), D((16,)), D((16,)), D((8,)), D((8,)), D((2,)), D((2,)), D((2,)), D((2,)),
+            D((5,)), D((16,)), D((16,)), D((8,)), D((8,)), D((4,)), D((4,)), D((16,)), D((16,)),
             D((1,)), D((1,)), D((4,)), D((4,)), D((4,)), D((4,)), D((4,)), D((4,)), D((4,)), D((4,)),
-            D((1,)), D((1,)), D((5,)),
+            D((1,)), D((1,)), D((11,)), pltpu.SemaphoreType.REGULAR,
         ],
         compiler_params=pltpu.CompilerParams(collective_id=0, has_side_effects=True, vmem_limit_bytes=60 * 2**20),
         name="attention_grads",
     )(key_lists, key_counts, queries, keys, values, grad_out, w_out)
-    dw = jnp.concatenate([dw[0].reshape(64, 128), dw[1].reshape(64, 128)], axis=1)
-    return dq, dk, dv, dw
+    return grads[0], grads[1], grads[2], dw
 
 
 def solution(mesh):

time: 72.7 us -> 61.9 us (0.85)
  Pallas kernels: 67.4 us -> 58.6 us
  local copies, waits for them, and re-layouts: 3.38 us -> 2.45 us
    pallas_call x1, Pallas kernels: 67.4 us -> 58.6 us  [shards(): pl.pallas_call(kernel, out_shape=(jax.ShapeDtypeStruct((3, 64, 1024), BF1...]
    unnamed x9 -> x3, local copies, waits for them, and re-layouts: 2.56 us -> 0.63 us
    squeeze x0 -> x1, local copies, waits for them, and re-layouts: none -> 1.81 us  [shards(): return (grads[0], grads[1], grads[2], dw)]
    slice x1 -> x0, local copies, waits for them, and re-layouts: 0.82 us -> none  [shards(): dw[0].reshape(64, 128)]
where the time goes in v3:
time: 61.9 us; the launch traced here: 61.7 us
  Pallas kernels  58.6 us (95%)
  local copies, waits for them, and re-layouts  2.45 us (4%)
  between operations  0.65 us (1%)
    pallas_call x1, Pallas kernels, shards(): pl.pallas_call(kernel, out_shape=(jax.ShapeDtypeStruct((3, 64, 1024), BF1...  58.6 us
    squeeze x1, local copies, waits for them, and re-layouts, shards(): return (grads[0], grads[1], grads[2], dw)  1.81 us

profile of v3, /device:TPU:1, one launch (start us, length us, event | category | flops | bytes accessed | tf_op | source)
XLA Modules:
  0.0 61.7 jit_solution(15278228647626548894)
XLA Ops:
  0.6 58.6 %attention_grads.1 = (bf16[3,64,1024]{2,1,0:T(8,128)(2,1)}, f32[64,256]{1,0:T(8,128)}) custom-call(s32[8,8]{1,0:T(8,128)} %lists.1, s32[8]{0:T(128)} %counts.1, bf16[64,1024]{1,0:T(8,128)(2,1)} %q_hbm.1, bf16[64,1024]{1,0:T(8,128)(2,1)} %k_hbm.1, bf16[64,1024]{1,0:T(8,128)(2,1)} %v_hbm.1, bf16[64,1024]{1,0:T(8,128)(2,1)} %g_hbm.1, bf16[64,256]{1,0:T(8,128)(2,1)} %w_hbm.1), custom_call_target="tpu_custom_call" | custom-call | tf_op jit(solution)/shard_map/attention_grads/pallas_call | solution.py:478
  59.3 0.0 copy-start
  59.3 1.8 %slice_bitcast_fusion = (bf16[64,1024]{1,0:T(8,128)(2,1)}, bf16[64,1024]{1,0:T(8,128)(2,1)}, bf16[64,1024]{1,0:T(8,128)(2,1)}) fusion(bf16[3,64,1024]{2,1,0:T(8,128)(2,1)} %get-tuple-element.6), kind=kLoop, calls=%fused_computation | loop fusion | bytes 786432 | tf_op jit(solution)/shard_map/squeeze | solution.py:499
  61.1 0.0 copy-done
  61.1 0.6 %copy.12 = f32[64,256]{1,0:T(8,128)} copy(f32[64,256]{1,0:T(8,128)S(1)} %copy-done) | data formatting | bytes 131072
Async XLA Ops:
  59.3 1.8 %copy-start = (f32[64,256]{1,0:T(8,128)S(1)}, f32[64,256]{1,0:T(8,128)}, u32[]{:S(2)}) copy-start(f32[64,256]{1,0:T(8,128)} %get-tuple-element.18) | copy-start | bytes 196612

commit v4 on v3

--- a/solution.py
+++ b/solution.py
@@ -119,11 +119,11 @@
     return pl.ds(pl.multiple_of(b * 128, 128), 128)
 
 
-def kernel(lists, counts, q_hbm, k_hbm, v_hbm, g_hbm, w_hbm, grads_hbm, dw_hbm,
-           eidx, inv_idx, bias, qv, kvb, gfull, wv, kv_fm, k_tm, v_tm, s_ref, p_ref, ps, inv_ref, att, acc, tmp,
-           dqv, dkv, halo_out, halo_in, pw, rc, xs, rx, mine, ry, ysum, rz, zsum, half, dwv,
+def kernel(lists_hbm, counts_hbm, q_hbm, k_hbm, v_hbm, g_hbm, w_hbm, grads_hbm, dw_hbm,
+           lists, counts, eidx, inv_idx, bias, qv, kvb, gfull, wv, kv_fm, k_tm, v_tm, s_ref, p_ref, ps, inv_ref, att, acc, tmp,
+           dqv, dkv, halo_out, halo_in, pw, rc, xs, rx, mine, ry, ysum, rz, zsum, half,
            load_sem, ag_send, ag_recv, fw_send, fw_recv, kv_send, kv_recv, ho_send, ho_recv,
-           c_send, c_recv, x_send, x_recv, y_send, y_recv, z_send, z_recv, a_send, a_recv, e_send, e_recv, out_sem, go):
+           c_send, c_recv, x_send, x_recv, y_send, y_recv, z_send, z_recv, a_send, a_recv, e_send, e_recv, out_sem):
     me = lax.axis_index("band")
     hi = lax.axis_index("head")
     core, x, y, z = lax.rem(me, 2), lax.rem(me // 2, 4), lax.rem(me // 8, 4), me // 32
@@ -146,8 +146,9 @@
         pl.semaphore_signal(barrier, inc=1, device_id={"band": b}, device_id_type=MESH)
     rows = pl.ds(pl.multiple_of(hi * 64, 64), 64)
     loads = [pltpu.make_async_copy(src, dst, load_sem.at[i]) for i, (src, dst) in enumerate([
-        (k_hbm, kvb.at[1, 0]), (v_hbm, kvb.at[1, 1]), (q_hbm, qv), (w_hbm, wv), (g_hbm, gfull.at[rows])])]
-    for c in loads:
+        (k_hbm, kvb.at[1, 0]), (v_hbm, kvb.at[1, 1]), (q_hbm, qv), (w_hbm, wv), (g_hbm, gfull.at[rows]),
+        (lists_hbm, lists), (counts_hbm, counts)])]
+    for c in loads[5:] + loads[:5]:
         c.start()
 
     column_low, column_high = x + y == 0, x + y == 6
@@ -192,6 +193,8 @@
                 t = jnp.where(es[j] == b + i, j, t)
             inv_idx[b * 17 + i] = t
         return 0
+    loads[5].wait()
+    loads[6].wait()
     lax.fori_loop(0, 8, table, 0)
     shape = (24, 128)
     pos = (first + lax.broadcasted_iota(jnp.int32, shape, 0)) * 128 + lax.broadcasted_iota(jnp.int32, shape, 1)
@@ -221,11 +224,7 @@
             for way in ways:
                 ag(c, way).start()
 
-    column = jnp.logical_or(x + y == 0, x + y == 6)
-    paired = jnp.logical_and(column, jnp.where(x == 0, z > 0, z < 3))
-    crossing = jnp.logical_and(paired, core == jnp.where(x == 0, 0, 1))
-    cross_low = jnp.logical_and(crossing, core == 0)
-    cross_high = jnp.logical_and(crossing, core == 1)
+    column = jnp.logical_or(column_low, column_high)
     pl.when(jnp.logical_not(column))(lambda: start_gather((0, 1)))
     pl.when(column_low)(lambda: start_gather((0,)))
     pl.when(column_high)(lambda: start_gather((1,)))
@@ -253,24 +252,15 @@
     keys_of(1)
     values_of(1)
 
-    pl.when(cross_low)(lambda: halo(2, 0).wait_send())
-    pl.when(cross_high)(lambda: halo(0, 0).wait_send())
-
-    @pl.when(crossing)
-    def _():
-        pl.semaphore_signal(go, inc=1, device_id={"band": other}, device_id_type=MESH)
-
-    @pl.when(jnp.logical_and(paired, jnp.logical_not(crossing)))
-    def _():
-        pl.semaphore_wait(go, 1)
-    pl.when(column_low)(lambda: start_gather((1,)))
-    pl.when(column_high)(lambda: start_gather((0,)))
-
     def arrived(side, i, prep):
         halo(side, i).wait_recv()
         prep(side)
-    pl.when(has_left)(lambda: arrived(0, 0, keys_of))
-    pl.when(has_right)(lambda: arrived(2, 0, keys_of))
+    pl.when(core == 0)(lambda: arrived(2, 0, keys_of))
+    pl.when(core == 1)(lambda: arrived(0, 0, keys_of))
+    pl.when(column_low)(lambda: start_gather((1,)))
+    pl.when(column_high)(lambda: start_gather((0,)))
+    pl.when(jnp.logical_and(core == 0, has_left))(lambda: arrived(0, 0, keys_of))
+    pl.when(jnp.logical_and(core == 1, has_right))(lambda: arrived(2, 0, keys_of))
 
     def ag_arrived(c, way):
         src = rows_from(way)
@@ -313,10 +303,15 @@
     x_copies = [remote(xs.at[x_of[d]], rx.at[d], x_send.at[d], x_recv.at[d], band=xs_ids[d]) for d in range(1, 4)]
     y_copies = [remote(mine, ry.at[d], y_send.at[d], y_recv.at[d], band=ys_ids[d]) for d in range(1, 4)]
     z_copies = [remote(ysum, rz.at[d], z_send.at[d], z_recv.at[d], band=zs_ids[d]) for d in range(1, 4)]
-    a_copies = [remote(zsum, half.at[x], a_send.at[d], a_recv.at[d], band=xs_ids[d]) for d in range(1, 4)]
-    a_waits = [remote(zsum, half.at[x_of[d]], a_send.at[d], a_recv.at[d], band=xs_ids[d]) for d in range(1, 4)]
-    e_copy = remote(half, dwv.at[core], e_send.at[0], e_recv.at[0], band=other)
-    e_wait = remote(half, dwv.at[give], e_send.at[0], e_recv.at[0], band=other)
+    my_rows = half.at[pl.ds(pl.multiple_of(x * 16, 16), 16)]
+    a_copies = [remote(zsum, my_rows, a_send.at[d], a_recv.at[d], band=xs_ids[d]) for d in range(1, 4)]
+    a_waits = [remote(zsum, half.at[pl.ds(pl.multiple_of(x_of[d] * 16, 16), 16)], a_send.at[d], a_recv.at[d], band=xs_ids[d]) for d in range(1, 4)]
+    def columns_of(c):
+        return dw_hbm.at[:, pl.ds(pl.multiple_of(c * 128, 128), 128)]
+
+    e_copy = remote(half, columns_of(core), e_send.at[0], e_recv.at[0], band=other)
+    e_wait = remote(half, columns_of(give), e_send.at[0], e_recv.at[0], band=other)
+    own_copy = pltpu.make_async_copy(half, columns_of(core), out_sem.at[3])
 
     def sum_core():
         total = dot_nt(att[...], gfull[...])
@@ -349,7 +344,7 @@
             c.wait_recv()
         t = ysum[...] + rz[1] + rz[2] + rz[3]
         zsum[...] = t
-        half[x] = t
+        my_rows[...] = t
         for c in a_copies:
             c.start()
 
@@ -357,7 +352,7 @@
         for c in a_waits:
             c.wait_recv()
         e_copy.start()
-        dwv[core] = half[...]
+        own_copy.start()
 
     def rest_of_chunk(c):
         ag_arrived(c, 1 - way_of(c)).wait_recv()
@@ -404,10 +399,11 @@
         lax.fori_loop(0, 8, send_upper, 0)
     outs = [pltpu.make_async_copy(dqv, grads_hbm.at[0], out_sem.at[0])]
     outs[0].start()
-    for step in ("core", "x", "y", "z"):
-        if step not in SUM_AT.values():
-            steps[step]()
+    for at, step in SUM_AT.items():
+        if START + at // 2 >= 8:
+            pl.when(start + at // 2 >= 8)(steps[step])
     gather_x()
+    gather_core()
 
     @pl.when(jnp.logical_not(has_right))
     def _():
@@ -428,13 +424,8 @@
     outs.append(pltpu.make_async_copy(dkv.at[64:128], grads_hbm.at[2], out_sem.at[2]))
     outs[1].start()
     outs[2].start()
-    gather_core()
     e_wait.wait_recv()
-    for i in range(2):
-        for r in range(4):
-            c = pltpu.make_async_copy(dwv.at[i, r], dw_hbm.at[r * 16:r * 16 + 16, i * 128:i * 128 + 128], out_sem.at[3 + i * 4 + r])
-            c.start()
-            outs.append(c)
+    own_copy.wait()
     for c in range(8):
         for way in range(2):
             ag(c, way).wait_send()
@@ -445,7 +436,7 @@
         for c in range(8):
             halo_back(0, c).wait_send()
 
-    pl.when(jnp.logical_and(has_left, jnp.logical_not(cross_low)))(lambda: halo(2, 0).wait_send())
+    pl.when(has_left)(lambda: halo(2, 0).wait_send())
     pl.when(has_left)(lambda: halo(2, 1).wait_send())
 
     @pl.when(has_right)
@@ -453,7 +444,7 @@
         for c in range(8):
             halo_back(1, c).wait_send()
 
-    pl.when(jnp.logical_and(has_right, jnp.logical_not(cross_high)))(lambda: halo(0, 0).wait_send())
+    pl.when(has_right)(lambda: halo(0, 0).wait_send())
     pl.when(has_right)(lambda: halo(0, 1).wait_send())
 
     for c in [core_copy] + x_copies + y_copies + z_copies + a_copies + [e_copy]:
@@ -464,38 +455,36 @@
 
 FORWARD_AT = {3: (0,), 5: (1,), 7: (2, 3)}
 FORWARD_LAST = (4, 5, 6, 7)
-START, START_LATE = 3, 3
-SUM_AT = {0: "core", 2: "x", 6: "y"}
+START, START_LATE = 3, 2
+SUM_AT = {0: "core", 2: "x", 6: "y", 10: "z"}
 
 
 def shards(queries, keys, values, grad_out, w_out, key_lists, key_counts):
     V, S, D = pltpu.VMEM, pltpu.SMEM, pltpu.SemaphoreType.DMA
     hbm = pl.BlockSpec(memory_space=pl.ANY)
-    smem = pl.BlockSpec(memory_space=S)
     slab = jax.ShapeDtypeStruct((64, 1024), BF16)
     piece = V((16, 128), F32)
     pieces = V((4, 16, 128), F32)
     grads, dw = pl.pallas_call(
         kernel,
         out_shape=(jax.ShapeDtypeStruct((3, 64, 1024), BF16), jax.ShapeDtypeStruct((64, 256), F32)),
-        in_specs=[smem, smem] + [hbm] * 5,
+        in_specs=[hbm] * 7,
         out_specs=[hbm] * 2,
         scratch_shapes=[
-            S((64,), jnp.int32), S((136,), jnp.int32), V((24, 128), F32), V((64, 1024), BF16),
+            S((8, 8), jnp.int32), S((8,), jnp.int32), S((64,), jnp.int32), S((136,), jnp.int32), V((24, 128), F32), V((64, 1024), BF16),
             V((3, 2, 64, 1024), BF16), V((256, 1024), BF16), V((64, 256), BF16),
             V((25, 128, 128), BF16), V((25, 128, 128), BF16), V((25, 128, 128), BF16),
             V((8, 128, 256), F32), V((64, 128, 256), F32), V((64, 128, 512), BF16), V((8, 1, 256), F32),
             V((64, 1024), BF16), V((24, 128, 128), F32), V((9, 128, 128), F32), V((64, 1024), BF16), V((128, 1024), BF16),
             V((2, 8, 128, 128), BF16), V((2, 8, 128, 128), BF16),
-            V((2, 64, 128), F32), V((64, 128), F32), pieces, pieces, piece, pieces, piece, pieces, piece, pieces,
-            V((2, 4, 16, 128), F32),
-            D((5,)), D((16,)), D((16,)), D((8,)), D((8,)), D((4,)), D((4,)), D((16,)), D((16,)),
+            V((2, 64, 128), F32), V((64, 128), F32), pieces, pieces, piece, pieces, piece, pieces, piece, V((64, 128), F32),
+            D((7,)), D((16,)), D((16,)), D((8,)), D((8,)), D((4,)), D((4,)), D((16,)), D((16,)),
             D((1,)), D((1,)), D((4,)), D((4,)), D((4,)), D((4,)), D((4,)), D((4,)), D((4,)), D((4,)),
-            D((1,)), D((1,)), D((11,)), pltpu.SemaphoreType.REGULAR,
+            D((1,)), D((1,)), D((4,)),
         ],
-        compiler_params=pltpu.CompilerParams(collective_id=0, has_side_effects=True, vmem_limit_bytes=60 * 2**20),
+        compiler_params=pltpu.CompilerParams(collective_id=0, has_side_effects=True, vmem_limit_bytes=36 * 2**20),
         name="attention_grads",
-    )(key_lists, key_counts, queries, keys, values, grad_out, w_out)
+    )(*[pltpu.with_memory_space_constraint(a, pltpu.HBM) for a in (key_lists, key_counts, queries, keys, values, grad_out, w_out)])
     return grads[0], grads[1], grads[2], dw
 
 

time: 61.9 us -> 61.1 us (0.987)
  local copies, waits for them, and re-layouts: 2.45 us -> 1.38 us
    squeeze x1, local copies, waits for them, and re-layouts: 1.81 us -> 0.75 us  [shards(): return (grads[0], grads[1], grads[2], dw)]
where the time goes in v4:
time: 61.1 us; the launch traced here: 60.9 us
  Pallas kernels  58.9 us (96%)
  local copies, waits for them, and re-layouts  1.38 us (2%)
  between operations  0.64 us (1%)
    pallas_call x1, Pallas kernels, shards(): pl.pallas_call(kernel, out_shape=(jax.ShapeDtypeStruct((3, 64, 1024), BF1...  58.9 us

profile of v4, /device:TPU:1, one launch (start us, length us, event | category | flops | bytes accessed | tf_op | source)
XLA Modules:
  0.0 60.9 jit_solution(1833724261560990723)
XLA Ops:
  0.6 58.9 %attention_grads.1 = (bf16[3,64,1024]{2,1,0:T(8,128)(2,1)S(1)}, f32[64,256]{1,0:T(8,128)S(1)}) custom-call(s32[8,8]{1,0:T(8,128)} %lists_hbm.1, s32[8]{0:T(128)} %counts_hbm.1, bf16[64,1024]{1,0:T(8,128)(2,1)} %q_hbm.1, bf16[64,1024]{1,0:T(8,128)(2,1)} %k_hbm.1, bf16[64,1024]{1,0:T(8,128)(2,1)} %v_hbm.1, bf16[64,1024]{1,0:T(8,128)(2,1)} %g_hbm.1, ...), custom_call_target="tpu_custom_call" | custom-call | tf_op jit(solution)/shard_map/attention_grads/pallas_call | solution.py:468
  59.6 0.8 %slice_bitcast_fusion = (bf16[64,1024]{1,0:T(8,128)(2,1)}, bf16[64,1024]{1,0:T(8,128)(2,1)}, bf16[64,1024]{1,0:T(8,128)(2,1)}) fusion(bf16[3,64,1024]{2,1,0:T(8,128)(2,1)S(1)} %get-tuple-element.6), kind=kLoop, calls=%fused_computation | loop fusion | bytes 786432 | tf_op jit(solution)/shard_map/squeeze | solution.py:488
  60.3 0.6 %copy.12 = f32[64,256]{1,0:T(8,128)} copy(f32[64,256]{1,0:T(8,128)S(1)} %get-tuple-element.18) | data formatting | bytes 131072

commit v5 on v4

--- a/solution.py
+++ b/solution.py
@@ -455,7 +455,7 @@
 
 FORWARD_AT = {3: (0,), 5: (1,), 7: (2, 3)}
 FORWARD_LAST = (4, 5, 6, 7)
-START, START_LATE = 3, 2
+START, START_LATE = 3, 1
 SUM_AT = {0: "core", 2: "x", 6: "y", 10: "z"}
 
 

time: 61.1 us -> 60.9 us (level)
  no operation moved by 1% of the time
where the time goes in v5:
time: 60.9 us; the launch traced here: 60.8 us
  Pallas kernels  58.7 us (96%)
  local copies, waits for them, and re-layouts  1.38 us (2%)
  between operations  0.64 us (1%)
    pallas_call x1, Pallas kernels, shards(): pl.pallas_call(kernel, out_shape=(jax.ShapeDtypeStruct((3, 64, 1024), BF1...  58.7 us

profile of v5, /device:TPU:1, one launch (start us, length us, event | category | flops | bytes accessed | tf_op | source)
XLA Modules:
  0.0 60.8 jit_solution(9593519295769248975)
XLA Ops:
  0.6 58.7 %attention_grads.1 = (bf16[3,64,1024]{2,1,0:T(8,128)(2,1)S(1)}, f32[64,256]{1,0:T(8,128)S(1)}) custom-call(s32[8,8]{1,0:T(8,128)} %lists_hbm.1, s32[8]{0:T(128)} %counts_hbm.1, bf16[64,1024]{1,0:T(8,128)(2,1)} %q_hbm.1, bf16[64,1024]{1,0:T(8,128)(2,1)} %k_hbm.1, bf16[64,1024]{1,0:T(8,128)(2,1)} %v_hbm.1, bf16[64,1024]{1,0:T(8,128)(2,1)} %g_hbm.1, ...), custom_call_target="tpu_custom_call" | custom-call | tf_op jit(solution)/shard_map/attention_grads/pallas_call | solution.py:468
  59.4 0.8 %slice_bitcast_fusion = (bf16[64,1024]{1,0:T(8,128)(2,1)}, bf16[64,1024]{1,0:T(8,128)(2,1)}, bf16[64,1024]{1,0:T(8,128)(2,1)}) fusion(bf16[3,64,1024]{2,1,0:T(8,128)(2,1)S(1)} %get-tuple-element.6), kind=kLoop, calls=%fused_computation | loop fusion | bytes 786432 | tf_op jit(solution)/shard_map/squeeze | solution.py:488
  60.1 0.6 %copy.12 = f32[64,256]{1,0:T(8,128)} copy(f32[64,256]{1,0:T(8,128)S(1)} %get-tuple-element.18) | data formatting | bytes 131072
